TPU v7x, 32 devices: a whole 2x2x4 slice. The times are simulated.
32 devices in a mesh: dp: 8 (over z, x), seq: 4 (over y, core).
Axes of the slice: x: 2, y: 2, z: 4, core: 2. Of those that a mesh axis runs over, the one named last changes fastest.
Arguments:
- tokens: float32 [16, 256, 1024], P('dp', 'seq'), may hold values from -6 to 6
- output_cotangent: float32 [16, 256, 1024], P('dp', 'seq'), may hold values from -0.5 to 0.5
- placement: int32 [8], replicated, may hold values from 0 to 15, as said below
- inward: float32 [1024, 3072], P(('dp', 'seq'))
- outward: float32 [1024, 1024], P(('dp', 'seq')), may hold values from -0.75 to 0.75
- attend_vectors: float32 [5, 1024], P(None, ('dp', 'seq'))
- expand: float32 [1024, 4096], P(('dp', 'seq')), may hold values from -0.1875 to 0.1875
- shrink: float32 [4096, 1024], P(('dp', 'seq')), may hold values from -0.09375 to 0.09375
- feed_vectors: float32 [3, 1024], P(None, ('dp', 'seq'))
- expand_bias: float32 [4096], P(('dp', 'seq')), may hold values from -3 to 3
- inward_moments: float32 [2, 1024, 3072], P(None, ('dp', 'seq')), as said below
- outward_moments: float32 [2, 1024, 1024], P(None, ('dp', 'seq'))
- attend_moments: float32 [2, 5, 1024], P(None, None, ('dp', 'seq'))
- expand_moments: float32 [2, 1024, 4096], P(None, ('dp', 'seq'))
- shrink_moments: float32 [2, 4096, 1024], P(None, ('dp', 'seq'))
- feed_moments: float32 [2, 3, 1024], P(None, None, ('dp', 'seq'))
- bias_moments: float32 [2, 4096], P(None, ('dp', 'seq'))
Outputs:
- block_output: float32 [16, 256, 1024], P('dp', 'seq')
- input_gradient: float32 [16, 256, 1024], P('dp', 'seq')
- inward_gradient: float32 [1024, 3072], P(('dp', 'seq'))
- outward_gradient: float32 [1024, 1024], P(('dp', 'seq'))
- attend_gradient: float32 [5, 1024], P(None, ('dp', 'seq'))
- expand_gradient: float32 [1024, 4096], P(('dp', 'seq'))
- shrink_gradient: float32 [4096, 1024], P(('dp', 'seq'))
- feed_gradient: float32 [3, 1024], P(None, ('dp', 'seq'))
- bias_gradient: float32 [4096], P(('dp', 'seq'))
- inward_new: float32 [1024, 3072], P(('dp', 'seq'))
- outward_new: float32 [1024, 1024], P(('dp', 'seq'))
- attend_new: float32 [5, 1024], P(None, ('dp', 'seq'))
- expand_new: float32 [1024, 4096], P(('dp', 'seq'))
- shrink_new: float32 [4096, 1024], P(('dp', 'seq'))
- feed_new: float32 [3, 1024], P(None, ('dp', 'seq'))
- bias_new: float32 [4096], P(('dp', 'seq'))
- inward_state: float32 [2, 1024, 3072], P(None, ('dp', 'seq'))
- outward_state: float32 [2, 1024, 1024], P(None, ('dp', 'seq'))
- attend_state: float32 [2, 5, 1024], P(None, None, ('dp', 'seq'))
- expand_state: float32 [2, 1024, 4096], P(None, ('dp', 'seq'))
- shrink_state: float32 [2, 4096, 1024], P(None, ('dp', 'seq'))
- feed_state: float32 [2, 3, 1024], P(None, None, ('dp', 'seq'))
- bias_state: float32 [2, 4096], P(None, ('dp', 'seq'))
Inputs may be any that keep to these rules, and one draw needn't show every extreme that they name: `placement`: entries are distinct slot numbers; slot s belongs to index s // 2 of dp; in every draw some index of dp holds 2 sequences. `inward_moments`: the second moment (index 1) is positive.
All inputs are finite; a program needn't handle non-finite values.
Results may differ from a plain program's by a relative error of at most 0.012.
Values may be sent and summed in bfloat16 or wider, within the bound.
A program may use at most 192 MiB of HBM per device.

v0:
```python
import math

import jax
import jax.numpy as jnp
from jax import lax
from jax.sharding import PartitionSpec as P

HEADS = 16
HEAD_DIM = 64


norm_epsilon = 1e-05
beta_first = 0.9
beta_second = 0.95
adam_epsilon = 1e-08
learn_rate = 0.01
weight_decay = 0.1
adam_steps = 4
gelu_scale = 0.7978845608028654
gelu_cubic = 0.044715
masked_score = -1e30


def halved(operand):
    return operand.astype(jnp.bfloat16)


def normalize(operand):
    average = jnp.mean(operand, axis=-1, keepdims=True)
    centered = operand - average
    variance = jnp.mean(centered * centered, axis=-1, keepdims=True)
    inverse = lax.rsqrt(variance + norm_epsilon)
    return (centered * inverse, inverse)


def norm_back(upstream, normed, inverse):
    first_mean = jnp.mean(upstream, axis=-1, keepdims=True)
    second_mean = jnp.mean(upstream * normed, axis=-1, keepdims=True)
    return inverse * (upstream - first_mean - normed * second_mean)


def gelu_pair(upper):
    inner_arg = gelu_scale * (upper + gelu_cubic * upper * upper * upper)
    tangent = jnp.tanh(inner_arg)
    active = 0.5 * upper * (1.0 + tangent)
    slope = 0.5 * (1.0 + tangent) + 0.5 * upper * (1.0 - tangent * tangent) * gelu_scale * (
        1.0 + 3.0 * gelu_cubic * upper * upper
    )
    return (active, slope)


def adamw_update(parameter, gradient, moments, decay_rate):
    first_moment = beta_first * moments[0] + (1.0 - beta_first) * gradient
    second = beta_second * moments[1] + (1.0 - beta_second) * gradient * gradient
    unbiased_first = first_moment / (1.0 - beta_first**adam_steps)
    unbiased_second = second / (1.0 - beta_second**adam_steps)
    update = unbiased_first / (jnp.sqrt(unbiased_second) + adam_epsilon) + decay_rate * parameter
    return (parameter - learn_rate * update, jnp.stack([first_moment, second]))


def lifted_fold(normed, pieces):
    weight_piece, vector_piece = pieces
    vector_float = vector_piece.astype(jnp.float32)
    lift_piece = halved(normed * vector_float[:, 0] + vector_float[:, 1])
    total = jnp.dot(lift_piece, weight_piece, preferred_element_type=jnp.float32)
    return (total, lift_piece, vector_float)


def body(
    tokens,
    output_cotangent,
    placement,
    inward,
    outward,
    attend_vectors,
    expand,
    shrink,
    feed_vectors,
    expand_bias,
    inward_moments,
    outward_moments,
    attend_moments,
    expand_moments,
    shrink_moments,
    feed_moments,
    bias_moments,
):
    slot_count, block_size, model_width = tokens.shape
    length = block_size * lax.axis_size("seq")
    row_count = slot_count * block_size
    score_scale = 1.0 / math.sqrt(HEAD_DIM)
    slot_ids = lax.axis_index("dp") * slot_count + jnp.arange(slot_count, dtype=jnp.int32)
    live_mask = jnp.any(placement[None, :] == slot_ids[:, None], axis=1).astype(jnp.float32)[
        :, None, None
    ]
    flat_tokens = tokens.reshape(row_count, model_width)
    normed_one, inverse_one = normalize(flat_tokens)
    attend_cols = halved(attend_vectors).T
    feed_cols = halved(feed_vectors).T
    packed, lifted_one, vec_rows_one = lifted_fold(
        normed_one,
        (
            lax.all_gather(halved(inward), ("dp", "seq"), axis=0, tiled=True),
            lax.all_gather(attend_cols, ("dp", "seq"), axis=0, tiled=True),
        ),
    )
    vec_one = vec_rows_one.T
    queries = halved(packed[:, :model_width] + vec_one[2]).reshape(
        slot_count, block_size, HEADS, HEAD_DIM
    )
    key_local = halved(packed[:, model_width : 2 * model_width]).reshape(
        slot_count, block_size, model_width
    )
    value_local = halved(packed[:, 2 * model_width :] + vec_one[3]).reshape(
        slot_count, block_size, model_width
    )
    key_whole, value_whole = (
        lax.all_gather(key_local, "seq", axis=1, tiled=True),
        lax.all_gather(value_local, "seq", axis=1, tiled=True),
    )
    key_heads = key_whole.reshape(slot_count, length, HEADS, HEAD_DIM)
    value_heads = value_whole.reshape(slot_count, length, HEADS, HEAD_DIM)
    query_pos = lax.axis_index("seq") * block_size + jnp.arange(block_size)
    allowed = jnp.arange(length)[None, :] <= query_pos[:, None]
    scores = (
        jnp.einsum("sqhd,skhd->shqk", queries, key_heads, preferred_element_type=jnp.float32)
        * score_scale
    )
    scores = jnp.where(allowed, scores, masked_score)
    score_peak = jnp.max(scores, axis=-1, keepdims=True)
    log_total = score_peak + jnp.log(jnp.sum(jnp.exp(scores - score_peak), axis=-1, keepdims=True))
    weights_half = halved(jnp.exp(scores - log_total))
    attended = halved(
        jnp.einsum(
            "shqk,skhd->sqhd", weights_half, value_heads, preferred_element_type=jnp.float32
        ).reshape(row_count, model_width)
    )
    projected = jnp.dot(
        attended,
        lax.all_gather(halved(outward), ("dp", "seq"), axis=0, tiled=True),
        preferred_element_type=jnp.float32,
    )
    middle = flat_tokens + projected + vec_one[4]
    normed_two, inverse_two = normalize(middle)
    upper_raw, lifted_two, vec_rows_two = lifted_fold(
        normed_two,
        (
            lax.all_gather(halved(expand), ("dp", "seq"), axis=0, tiled=True),
            lax.all_gather(feed_cols, ("dp", "seq"), axis=0, tiled=True),
        ),
    )
    vec_two = vec_rows_two.T
    weight_piece = lax.all_gather(halved(shrink), ("dp", "seq"), axis=0, tiled=True)
    bias_piece = lax.all_gather(halved(expand_bias), ("dp", "seq"), axis=0, tiled=True)
    bias_float = bias_piece.astype(jnp.float32)
    upper_cols = upper_raw + bias_float
    act_cols, unused_slope = gelu_pair(upper_cols)
    act_half = halved(act_cols)
    total = jnp.dot(act_half, weight_piece, preferred_element_type=jnp.float32)
    upper_act = upper_raw + bias_float
    unused_active, gelu_slope = gelu_pair(upper_act)
    result = middle + total + vec_two[2]
    block_output = result.reshape(slot_count, block_size, model_width) * live_mask
    cotangent = (output_cotangent * live_mask).reshape(row_count, model_width)
    cot_half = halved(cotangent)
    shrink_grad = jnp.dot(act_half.T, cot_half, preferred_element_type=jnp.float32)
    feed_bias_grad = jnp.sum(cotangent, axis=0)
    upper_grad = (
        jnp.dot(
            cot_half,
            lax.all_gather(halved(shrink), ("dp", "seq"), axis=0, tiled=True).T,
            preferred_element_type=jnp.float32,
        )
        * gelu_slope
    )
    upper_half = halved(upper_grad)
    expand_grad = jnp.dot(lifted_two.T, upper_half, preferred_element_type=jnp.float32)
    expand_bias_grad = jnp.sum(upper_grad, axis=0)
    lift_two_grad = jnp.dot(
        upper_half,
        lax.all_gather(halved(expand), ("dp", "seq"), axis=0, tiled=True).T,
        preferred_element_type=jnp.float32,
    )
    gain_two_grad = jnp.sum(lift_two_grad * normed_two, axis=0)
    shift_two_grad = jnp.sum(lift_two_grad, axis=0)
    middle_grad = cotangent + norm_back(lift_two_grad * vec_two[0], normed_two, inverse_two)
    feed_vec_grad = jnp.stack([gain_two_grad, shift_two_grad, feed_bias_grad], axis=1)
    feed_parts = (
        lax.psum_scatter(expand_grad, ("dp", "seq"), scatter_dimension=0, tiled=True),
        lax.psum_scatter(shrink_grad, ("dp", "seq"), scatter_dimension=0, tiled=True),
        lax.psum_scatter(feed_vec_grad, ("dp", "seq"), scatter_dimension=0, tiled=True),
        lax.psum_scatter(expand_bias_grad, ("dp", "seq"), scatter_dimension=0, tiled=True),
    )
    middle_half = halved(middle_grad)
    outward_grad = jnp.dot(attended.T, middle_half, preferred_element_type=jnp.float32)
    out_bias_grad = jnp.sum(middle_grad, axis=0)
    attended_back = jnp.dot(
        middle_half,
        lax.all_gather(halved(outward), ("dp", "seq"), axis=0, tiled=True).T,
        preferred_element_type=jnp.float32,
    )
    attended_grad = halved(attended_back).reshape(slot_count, block_size, HEADS, HEAD_DIM)
    attended_heads = attended.reshape(slot_count, block_size, HEADS, HEAD_DIM)
    delta_sum = jnp.sum(
        attended_grad.astype(jnp.float32) * attended_heads.astype(jnp.float32), axis=-1
    )
    scores_again = (
        jnp.einsum("sqhd,skhd->shqk", queries, key_heads, preferred_element_type=jnp.float32)
        * score_scale
    )
    scores_again = jnp.where(allowed, scores_again, masked_score)
    weights_full = jnp.exp(scores_again - log_total)
    weights_again = halved(weights_full)
    weight_grad = jnp.einsum(
        "sqhd,skhd->shqk", attended_grad, value_heads, preferred_element_type=jnp.float32
    )
    score_grad = halved(
        weights_full * (weight_grad - jnp.transpose(delta_sum, (0, 2, 1))[..., None]) * score_scale
    )
    query_grad = jnp.einsum(
        "shqk,skhd->sqhd", score_grad, key_heads, preferred_element_type=jnp.float32
    ).reshape(row_count, model_width)
    key_term = jnp.einsum(
        "shqk,sqhd->skhd", score_grad, queries, preferred_element_type=jnp.float32
    ).reshape(slot_count, length, model_width)
    value_term = jnp.einsum(
        "shqk,sqhd->skhd", weights_again, attended_grad, preferred_element_type=jnp.float32
    ).reshape(slot_count, length, model_width)
    key_grad, value_grad = (
        lax.psum_scatter(
            key_term.astype(jnp.bfloat16), "seq", scatter_dimension=1, tiled=True
        ).astype(jnp.float32),
        lax.psum_scatter(
            value_term.astype(jnp.bfloat16), "seq", scatter_dimension=1, tiled=True
        ).astype(jnp.float32),
    )
    key_grad = key_grad.reshape(row_count, model_width)
    value_grad = value_grad.reshape(row_count, model_width)
    packed_grad = halved(jnp.concatenate([query_grad, key_grad, value_grad], axis=1))
    inward_grad = jnp.dot(lifted_one.T, packed_grad, preferred_element_type=jnp.float32)
    query_bias_grad = jnp.sum(query_grad, axis=0)
    value_bias_grad = jnp.sum(value_grad, axis=0)
    lift_one_grad = jnp.dot(
        packed_grad,
        lax.all_gather(halved(inward), ("dp", "seq"), axis=0, tiled=True).T,
        preferred_element_type=jnp.float32,
    )
    gain_one_grad = jnp.sum(lift_one_grad * normed_one, axis=0)
    shift_one_grad = jnp.sum(lift_one_grad, axis=0)
    tokens_grad = middle_grad + norm_back(lift_one_grad * vec_one[0], normed_one, inverse_one)
    input_gradient = tokens_grad.reshape(slot_count, block_size, model_width) * live_mask
    attend_vec_grad = jnp.stack(
        [gain_one_grad, shift_one_grad, query_bias_grad, value_bias_grad, out_bias_grad], axis=1
    )
    attend_parts = (
        lax.psum_scatter(inward_grad, ("dp", "seq"), scatter_dimension=0, tiled=True),
        lax.psum_scatter(outward_grad, ("dp", "seq"), scatter_dimension=0, tiled=True),
        lax.psum_scatter(attend_vec_grad, ("dp", "seq"), scatter_dimension=0, tiled=True),
    )
    attend_vec_sum = attend_parts[2].T
    feed_vec_sum = feed_parts[2].T
    inward_new, inward_state = adamw_update(inward, attend_parts[0], inward_moments, weight_decay)
    outward_new, outward_state = adamw_update(
        outward, attend_parts[1], outward_moments, weight_decay
    )
    attend_new, attend_state = adamw_update(attend_vectors, attend_vec_sum, attend_moments, 0.0)
    expand_new, expand_state = adamw_update(expand, feed_parts[0], expand_moments, weight_decay)
    shrink_new, shrink_state = adamw_update(shrink, feed_parts[1], shrink_moments, weight_decay)
    feed_new, feed_state = adamw_update(feed_vectors, feed_vec_sum, feed_moments, 0.0)
    bias_new, bias_state = adamw_update(expand_bias, feed_parts[3], bias_moments, 0.0)
    return (
        block_output,
        input_gradient,
        attend_parts[0],
        attend_parts[1],
        attend_vec_sum,
        feed_parts[0],
        feed_parts[1],
        feed_vec_sum,
        feed_parts[3],
        inward_new,
        outward_new,
        attend_new,
        expand_new,
        shrink_new,
        feed_new,
        bias_new,
        inward_state,
        outward_state,
        attend_state,
        expand_state,
        shrink_state,
        feed_state,
        bias_state,
    )


def solution(mesh):
    placed = (
        P("dp", "seq", None),
        P("dp", "seq", None),
        P(),
        P(("dp", "seq"), None),
        P(("dp", "seq"), None),
        P(None, ("dp", "seq")),
        P(("dp", "seq"), None),
        P(("dp", "seq"), None),
        P(None, ("dp", "seq")),
        P(("dp", "seq")),
        P(None, ("dp", "seq"), None),
        P(None, ("dp", "seq"), None),
        P(None, None, ("dp", "seq")),
        P(None, ("dp", "seq"), None),
        P(None, ("dp", "seq"), None),
        P(None, None, ("dp", "seq")),
        P(None, ("dp", "seq")),
    )
    return jax.shard_map(
        body,
        mesh=mesh,
        in_specs=placed,
        out_specs=(
            P("dp", "seq", None),
            P("dp", "seq", None),
            P(("dp", "seq"), None),
            P(("dp", "seq"), None),
            P(None, ("dp", "seq")),
            P(("dp", "seq"), None),
            P(("dp", "seq"), None),
            P(None, ("dp", "seq")),
            P(("dp", "seq")),
            P(("dp", "seq"), None),
            P(("dp", "seq"), None),
            P(None, ("dp", "seq")),
            P(("dp", "seq"), None),
            P(("dp", "seq"), None),
            P(None, ("dp", "seq")),
            P(("dp", "seq")),
            P(None, ("dp", "seq"), None),
            P(None, ("dp", "seq"), None),
            P(None, None, ("dp", "seq")),
            P(None, ("dp", "seq"), None),
            P(None, ("dp", "seq"), None),
            P(None, None, ("dp", "seq")),
            P(None, ("dp", "seq")),
        ),
        check_vma=False,
    )
```

profile of v0, /device:TPU:0, one launch (start us, length us, event | category | flops | bytes accessed | tf_op | source)
XLA Modules:
  0.0 1383.9 jit_solution(13482467230646633061)
XLA Ops:
  9.8 43.8 %all-gather = bf16[32,32,5]{1,2,0:T(8,128)(2,1)S(1)} all-gather(bf16[1,32,5]{1,2,0:T(8,128)(2,1)S(1)} %convert_bitcast_fusion), channel_id=1, replica_groups=mesh['dp'=8,'seq'=4] {'dp','seq'}, dimensions={0}, use_global_device_ids=true | all-gather | bytes 10560 | tf_op jit(solution)/shard_map/all_gather | solution.py:104
  57.0 26.5 %all-gather.10.cloned.1.call-done = bf16[1024,3072]{1,0:T(8,128)(2,1)} async-done(((bf16[32,3072]{1,0:T(8,128)(2,1)}), bf16[1024,3072]{1,0:T(8,128)(2,1)}) %all-gather.10.cloned.1.call-update) | async-done | bytes 6291472 | tf_op jit(solution)/shard_map/all_gather | solution.py:103
  83.6 3.8 fusion.61
  90.7 39.1 %all-gather.1 = bf16[32,32,3]{1,2,0:T(4,128)(2,1)S(1)} all-gather(bf16[1,32,3]{1,2,0:T(4,128)(2,1)S(1)} %convert_bitcast_fusion.1), channel_id=1, replica_groups=mesh['dp'=8,'seq'=4] {'dp','seq'}, dimensions={0}, use_global_device_ids=true | all-gather | bytes 6336 | tf_op jit(solution)/shard_map/all_gather | solution.py:149
  129.9 36.7 %all-gather.2 = bf16[32,1,128]{2,1,0:T(2,128)(2,1)S(1)} all-gather(bf16[1,1,128]{2,1,0:T(2,128)(2,1)S(1)} %convert_bitcast_fusion.2), channel_id=1, replica_groups=mesh['dp'=8,'seq'=4] {'dp','seq'}, dimensions={0}, use_global_device_ids=true | all-gather | bytes 8448 | tf_op jit(solution)/shard_map/all_gather | solution.py:154
  171.3 2.4 copy.101
  173.8 2.3 copy.102
  185.6 75.8 %all-gather.18.cloned.1.call-done = bf16[1024,4096]{1,0:T(8,128)(2,1)} async-done(((bf16[32,4096]{1,0:T(8,128)(2,1)}), bf16[1024,4096]{1,0:T(8,128)(2,1)}) %all-gather.18.cloned.1.call-update) | async-done | bytes 8388624 | tf_op jit(solution)/shard_map/all_gather | solution.py:148
  261.5 4.8 convolution_add_fusion
  267.6 8.1 fusion.49
  275.8 182.0 %reduce-scatter.23.cloned.1.call-done = f32[128,1024]{1,0:T(8,128)} async-done(((f32[4096,1024]{1,0:T(8,128)}), f32[128,1024]{1,0:T(8,128)}) %reduce-scatter.23.cloned.1.call-update) | async-done | bytes 524304 | tf_op jit(solution)/shard_map/reduce_scatter | solution.py:190
  457.8 3.2 fusion.24
  462.6 77.1 %all-gather.20.cloned.1.call-done = bf16[4096,1024]{1,0:T(8,128)(2,1)} async-done(((bf16[128,1024]{1,0:T(8,128)(2,1)}), bf16[4096,1024]{1,0:T(8,128)(2,1)}) %all-gather.20.cloned.1.call-update) | async-done | bytes 8388624 | tf_op jit(solution)/shard_map/all_gather | solution.py:153
  539.7 8.3 fusion.60
  548.0 7.4 multiply_reduce_fusion.1
  563.0 2.6 convolution_convert_fusion
  565.5 2.3 copy.112
  574.0 2.4 copy.110
  579.8 11.6 reduce-scatter.15.cloned.1.call-done
  591.4 27.4 %reduce-scatter.13.cloned.1.call-done = bf16[2,64,1024]{2,1,0:T(8,128)(2,1)} async-done(((bf16[2,256,1024]{2,1,0:T(8,128)(2,1)}), bf16[2,64,1024]{2,1,0:T(8,128)(2,1)}) %reduce-scatter.13.cloned.1.call-update) | async-done | bytes 262160 | tf_op jit(solution)/shard_map/reduce_scatter | solution.py:230
  618.8 6.1 multiply_reduce_fusion.2
  626.1 2.7 fusion.26
  629.8 6.3 fusion.19
  637.4 8.2 fusion.14
  646.3 2.3 pad_maximum_fusion.1
  648.6 39.4 %all-reduce = f32[4096]{0:T(1024)S(1)} all-reduce(f32[4096]{0:T(1024)S(1)} %copy-done.42), channel_id=10, replica_groups=mesh['dp'=8,'seq'=4] {'dp','seq'}, use_global_device_ids=true, to_apply=%region_29.30.clone | all-reduce | flops 4096 | bytes 32768
  689.2 5.7 fusion.8
  694.9 61.8 %reduce-scatter.27.cloned.1.call-done = f32[32,3]{1,0:T(8,128)} async-done(((f32[1024,3]{1,0:T(8,128)}), f32[32,3]{1,0:T(8,128)}) %reduce-scatter.27.cloned.1.call-update) | async-done | bytes 400
  761.5 129.5 %reduce-scatter.25.cloned.1.call-done = f32[32,5]{1,0:T(8,128)} async-done(((f32[1024,5]{1,0:T(8,128)}), f32[32,5]{1,0:T(8,128)}) %reduce-scatter.25.cloned.1.call-update) | async-done | bytes 656
  893.0 138.8 %reduce-scatter.19.cloned.1.call-done = f32[32,1024]{1,0:T(8,128)} async-done(((f32[1024,1024]{1,0:T(8,128)}), f32[32,1024]{1,0:T(8,128)}) %reduce-scatter.19.cloned.1.call-update) | async-done | bytes 131088 | tf_op jit(solution)/shard_map/reduce_scatter | solution.py:257
  1034.2 155.0 %reduce-scatter.17.cloned.1.call-done = f32[32,3072]{1,0:T(8,128)} async-done(((f32[1024,3072]{1,0:T(8,128)}), f32[32,3072]{1,0:T(8,128)}) %reduce-scatter.17.cloned.1.call-update) | async-done | bytes 393232 | tf_op jit(solution)/shard_map/reduce_scatter | solution.py:256
  1192.2 182.0 %reduce-scatter.21.cloned.1.call-done = f32[32,4096]{1,0:T(8,128)} async-done(((f32[1024,4096]{1,0:T(8,128)}), f32[32,4096]{1,0:T(8,128)}) %reduce-scatter.21.cloned.1.call-update) | async-done | bytes 524304 | tf_op jit(solution)/shard_map/reduce_scatter | solution.py:189
  (238 shorter events, 64.1 us)
Async XLA Ops:
  7.2 49.7 %copy-start = (f32[2,64,1024]{2,1,0:T(8,128)S(1)}, f32[2,64,1024]{2,1,0:T(8,128)}, u32[]{:S(2)}) copy-start(f32[2,64,1024]{2,1,0:T(8,128)} %param.17) | copy-start | bytes 1572868
  7.2 76.4 %all-gather.10.cloned.1.call-start = ((), (), s32[]{:S(2)}) async-start(), calls=%async_computation.8 | async-start | bytes 6488064 | tf_op jit(solution)/shard_map/all_gather | solution.py:103
  9.0 162.3 %all-gather.12.cloned.1.call-start = ((), (), s32[]{:S(2)}) async-start(), calls=%async_computation.9 | async-start | bytes 1310720 | tf_op jit(solution)/shard_map/all_gather | solution.py:119
  87.4 79.9 %copy-start.61 = (s32[8]{0:T(128)S(1)}, s32[8]{0:T(128)}, u32[]{:S(2)}) copy-start(s32[8]{0:T(128)} %param.19) | copy-start | bytes 100
  88.2 85.5 %all-gather.14.cloned.1.call-start = ((), (), s32[]{:S(2)}) async-start(), calls=%async_computation.10 | async-start | bytes 1310720 | tf_op jit(solution)/shard_map/all_gather | solution.py:118
  89.0 79.1 %copy-start.27 = (f32[2,64,1024]{2,1,0:T(8,128)S(1)}, f32[2,64,1024]{2,1,0:T(8,128)}, u32[]{:S(2)}) copy-start(f32[2,64,1024]{2,1,0:T(8,128)} %param.18) | copy-start | bytes 1572868
  89.1 94.1 %all-gather.16.cloned.1.call-start = ((), (), s32[]{:S(2)}) async-start(), calls=%async_computation.11 | async-start | bytes 2162688 | tf_op jit(solution)/shard_map/all_gather | solution.py:140
  89.8 171.7 %all-gather.18.cloned.1.call-start = ((), (), s32[]{:S(2)}) async-start(), calls=%async_computation.12 | async-start | bytes 8650752 | tf_op jit(solution)/shard_map/all_gather | solution.py:148
  90.6 367.2 %reduce-scatter.23.cloned.1.call-start = ((), (), s32[]{:S(2)}) async-start(), calls=%async_computation.19 | async-start | bytes 17301504 | tf_op jit(solution)/shard_map/reduce_scatter | solution.py:190
  185.4 370.0 %copy-start.32 = (f32[128]{0:T(128)}, f32[128]{0:T(128)S(1)}, u32[]{:S(2)}) copy-start(f32[128]{0:T(128)S(1)} %broadcast_multiply_fusion.8) | copy-start | bytes 1540
  185.6 80.6 %copy-start.34 = (f32[128]{0:T(128)}, f32[128]{0:T(128)S(1)}, u32[]{:S(2)}) copy-start(f32[128]{0:T(128)S(1)} %add_rsqrt_fusion.1) | copy-start | bytes 1540
  275.8 263.9 %all-gather.20.cloned.1.call-start = ((), (), s32[]{:S(2)}) async-start(), calls=%async_computation.13 | async-start | bytes 8650752 | tf_op jit(solution)/shard_map/all_gather | solution.py:153
  461.0 130.4 %reduce-scatter.15.cloned.1.call-start = ((), (), s32[]{:S(2)}) async-start(), calls=%async_computation.15 | async-start | bytes 1310720 | tf_op jit(solution)/shard_map/reduce_scatter | solution.py:233
  567.8 50.9 %reduce-scatter.13.cloned.1.call-start = ((), (), s32[]{:S(2)}) async-start(), calls=%async_computation.14 | async-start | bytes 1310720 | tf_op jit(solution)/shard_map/reduce_scatter | solution.py:230
  576.4 180.3 %reduce-scatter.27.cloned.1.call-start = ((), (), s32[]{:S(2)}) async-start(), calls=%async_computation.21 | async-start | bytes 540672
  579.5 311.5 %reduce-scatter.25.cloned.1.call-start = ((), (), s32[]{:S(2)}) async-start(), calls=%async_computation.20 | async-start | bytes 540672
  626.0 405.8 %reduce-scatter.19.cloned.1.call-start = ((), (), s32[]{:S(2)}) async-start(), calls=%async_computation.17 | async-start | bytes 4325376 | tf_op jit(solution)/shard_map/reduce_scatter | solution.py:257
  628.9 560.3 %reduce-scatter.17.cloned.1.call-start = ((), (), s32[]{:S(2)}) async-start(), calls=%async_computation.16 | async-start | bytes 12976128 | tf_op jit(solution)/shard_map/reduce_scatter | solution.py:256
  636.2 738.0 %reduce-scatter.21.cloned.1.call-start = ((), (), s32[]{:S(2)}) async-start(), calls=%async_computation.18 | async-start | bytes 17301504 | tf_op jit(solution)/shard_map/reduce_scatter | solution.py:189
  689.1 68.4 %copy-start.45 = (f32[3,32]{1,0:T(4,128)S(1)}, f32[3,32]{1,0:T(4,128)}, u32[]{:S(2)}) copy-start(f32[3,32]{1,0:T(4,128)} %param.25) | copy-start | bytes 1156
  689.1 69.6 %copy-start.38 = (f32[1,1024]{1,0:T(1,128)S(1)}, f32[1,1024]{1,0:T(1,128)}, u32[]{:S(2)}) copy-start(f32[1,1024]{1,0:T(1,128)} %get-tuple-element.169) | copy-start | bytes 12292
  689.2 69.6 %copy-start.52 = (f32[128]{0:T(128)S(1)}, f32[128]{0:T(128)}, u32[]{:S(2)}) copy-start(f32[128]{0:T(128)} %copy-done.50) | copy-start | bytes 1540
  689.2 69.6 %copy-start.55 = (f32[128]{0:T(128)S(1)}, f32[128]{0:T(128)}, u32[]{:S(2)}) copy-start(f32[128]{0:T(128)} %copy-done.53) | copy-start | bytes 1540
  694.9 65.4 %copy-start.25 = (f32[128,1024]{1,0:T(8,128)S(1)}, f32[128,1024]{1,0:T(8,128)}, u32[]{:S(2)}) copy-start(f32[128,1024]{1,0:T(8,128)} %fusion.8) | copy-start | bytes 1572868
  694.9 65.4 %copy-start.57 = (f32[2]{0:T(128)S(1)}, f32[2]{0:T(128)}, u32[]{:S(2)}) copy-start(f32[2]{0:T(128)} %copy-done.56) | copy-start | bytes 28
  758.8 133.0 %copy-start.41 = (f32[5,32]{1,0:T(8,128)S(1)}, f32[5,32]{1,0:T(8,128)}, u32[]{:S(2)}) copy-start(f32[5,32]{1,0:T(8,128)} %param.22) | copy-start | bytes 1924
  758.8 273.1 %copy-start.29 = (f32[2,32,1024]{2,1,0:T(8,128)S(1)}, f32[2,32,1024]{2,1,0:T(8,128)}, u32[]{:S(2)}) copy-start(f32[2,32,1024]{2,1,0:T(8,128)} %param.28) | copy-start | bytes 786436
  760.3 428.9 %copy-start.20 = (f32[32,3072]{1,0:T(8,128)S(1)}, f32[32,3072]{1,0:T(8,128)}, u32[]{:S(2)}) copy-start(f32[32,3072]{1,0:T(8,128)} %param.20) | copy-start | bytes 1179652
  760.3 428.9 %copy-start.24 = (f32[2,32,3072]{2,1,0:T(8,128)S(1)}, f32[2,32,3072]{2,1,0:T(8,128)}, u32[]{:S(2)}) copy-start(f32[2,32,3072]{2,1,0:T(8,128)} %param.27) | copy-start | bytes 2359300
  891.8 299.5 %copy-start.40 = (f32[32,5]{0,1:T(8,128)}, f32[32,5]{0,1:T(8,128)S(1)}, u32[]{:S(2)}) copy-start(f32[32,5]{0,1:T(8,128)S(1)} %copy.118) | copy-start | bytes 1924
  1034.2 339.9 %copy-start.19 = (f32[32,4096]{1,0:T(8,128)S(1)}, f32[32,4096]{1,0:T(8,128)}, u32[]{:S(2)}) copy-start(f32[32,4096]{1,0:T(8,128)} %param.23) | copy-start | bytes 1572868
  1034.2 339.9 %copy-start.22 = (f32[2,32,4096]{2,1,0:T(8,128)S(1)}, f32[2,32,4096]{2,1,0:T(8,128)}, u32[]{:S(2)}) copy-start(f32[2,32,4096]{2,1,0:T(8,128)} %param.30) | copy-start | bytes 3145732
  (44 other events, 502.2 us)
Sparse Core Ops, SparseCore 0:
  11.5 72.0 all-gather.9
  88.4 15.2 all-gather.11
  105.8 16.7 all-gather.13
  125.9 56.2 all-gather.15
  185.5 75.9 all-gather.17
  275.9 181.8 reduce-scatter.22
  461.2 78.4 all-gather.19
  567.9 23.4 reduce-scatter.14
  593.9 24.7 reduce-scatter.12
  620.8 135.8 reduce-scatter.26
  759.6 131.3 reduce-scatter.24
  893.7 138.1 reduce-scatter.18
  1038.4 150.7 reduce-scatter.16
  1191.9 182.1 reduce-scatter.20
where the time goes:
time: 1390 us; the launch traced here: 1380 us
  waiting for transfers between devices  1070 us (77%)
  blocking collectives  159 us (11%)
  matrix products  74.3 us (5%)
  local copies, waits for them, and re-layouts  34.1 us (2%)
  other arithmetic  33.4 us (2%)
  between operations  14.6 us (1%)
    unnamed x16, waiting for transfers between devices  192 us
    reduce_scatter x1, waiting for transfers between devices, body(): lax.psum_scatter(shrink_grad, ('dp', 'seq'), scatter_dimension=0, tiled=T...  182 us
    reduce_scatter x1, waiting for transfers between devices, body(): lax.psum_scatter(expand_grad, ('dp', 'seq'), scatter_dimension=0, tiled=T...  182 us
    reduce_scatter x1, waiting for transfers between devices, body(): lax.psum_scatter(inward_grad, ('dp', 'seq'), scatter_dimension=0, tiled=T...  155 us
    reduce_scatter x1, waiting for transfers between devices, body(): lax.psum_scatter(outward_grad, ('dp', 'seq'), scatter_dimension=0, tiled=...  139 us
    all_gather x1, waiting for transfers between devices, body(): lax.all_gather(halved(shrink), ('dp', 'seq'), axis=0, tiled=True)  77.1 us
    all_gather x1, waiting for transfers between devices, body(): lax.all_gather(halved(expand), ('dp', 'seq'), axis=0, tiled=True)  75.8 us
    all_gather x1, blocking collectives, body(): lax.all_gather(attend_cols, ('dp', 'seq'), axis=0, tiled=True)  43.8 us
  transfers between devices with their start and end apart: 14, of which 11 were waited for; matrix products, arithmetic and copies ran while one was open for 6% of the time, Pallas kernels for 0%

commit v1 on v0

v1 whole, which is shorter than its diff:
```python
import math

import jax
import jax.numpy as jnp
from jax import lax
from jax.sharding import PartitionSpec as P

HEADS = 16
HEAD_DIM = 64


norm_epsilon = 1e-05
beta_first = 0.9
beta_second = 0.95
adam_epsilon = 1e-08
learn_rate = 0.01
weight_decay = 0.1
adam_steps = 4
gelu_scale = 0.7978845608028654
gelu_cubic = 0.044715
masked_score = -1e30


def halved(operand):
    return operand.astype(jnp.bfloat16)


def normalize(operand):
    average = jnp.mean(operand, axis=-1, keepdims=True)
    centered = operand - average
    variance = jnp.mean(centered * centered, axis=-1, keepdims=True)
    inverse = lax.rsqrt(variance + norm_epsilon)
    return (centered * inverse, inverse)


def norm_back(upstream, normed, inverse):
    first_mean = jnp.mean(upstream, axis=-1, keepdims=True)
    second_mean = jnp.mean(upstream * normed, axis=-1, keepdims=True)
    return inverse * (upstream - first_mean - normed * second_mean)


def gelu_pair(upper):
    inner_arg = gelu_scale * (upper + gelu_cubic * upper * upper * upper)
    tangent = jnp.tanh(inner_arg)
    active = 0.5 * upper * (1.0 + tangent)
    slope = 0.5 * (1.0 + tangent) + 0.5 * upper * (1.0 - tangent * tangent) * gelu_scale * (
        1.0 + 3.0 * gelu_cubic * upper * upper
    )
    return (active, slope)


def adamw_update(parameter, gradient, moments, decay_rate):
    first_moment = beta_first * moments[0] + (1.0 - beta_first) * gradient
    second = beta_second * moments[1] + (1.0 - beta_second) * gradient * gradient
    unbiased_first = first_moment / (1.0 - beta_first**adam_steps)
    unbiased_second = second / (1.0 - beta_second**adam_steps)
    update = unbiased_first / (jnp.sqrt(unbiased_second) + adam_epsilon) + decay_rate * parameter
    return (parameter - learn_rate * update, jnp.stack([first_moment, second]))


def spread_columns(piece, groups, inner):
    rows = piece.shape[0]
    parts = piece.reshape(rows, -1, groups, inner)
    moved = lax.all_to_all(parts, "seq", 2, 0, tiled=True)
    return moved.reshape(groups * rows, -1)


def collect_columns(piece, groups, inner):
    rows = piece.shape[0] // groups
    parts = piece.reshape(rows * groups, -1, 1, inner)
    moved = lax.all_to_all(parts, "seq", 0, 2, tiled=True)
    return moved.reshape(rows, -1)


def body(
    tokens,
    output_cotangent,
    placement,
    inward,
    outward,
    attend_vectors,
    expand,
    shrink,
    feed_vectors,
    expand_bias,
    inward_moments,
    outward_moments,
    attend_moments,
    expand_moments,
    shrink_moments,
    feed_moments,
    bias_moments,
):
    slot_count, block_size, model_width = tokens.shape
    groups = lax.axis_size("seq")
    replicas = lax.axis_size("dp")
    devices = groups * replicas
    mine = lax.axis_index("seq")
    length = block_size * groups
    row_count = slot_count * block_size
    all_rows = slot_count * length
    head_count = HEADS // groups
    part_width = head_count * HEAD_DIM
    vec_width = attend_vectors.shape[1]
    hidden_part = expand_bias.shape[0]
    score_scale = 1.0 / math.sqrt(HEAD_DIM)
    whole = ("dp", "seq")

    def gather_rows(local):
        full = lax.all_gather(
            local.reshape(slot_count, block_size, -1), "seq", axis=1, tiled=True
        )
        return full.reshape(all_rows, -1)

    def scatter_rows(partial):
        own = lax.psum_scatter(
            halved(partial).reshape(slot_count, length, -1), "seq", scatter_dimension=1, tiled=True
        )
        return own.reshape(row_count, -1).astype(jnp.float32)

    slot_ids = lax.axis_index("dp") * slot_count + jnp.arange(slot_count, dtype=jnp.int32)
    live_mask = jnp.any(placement[None, :] == slot_ids[:, None], axis=1).astype(jnp.float32)[
        :, None, None
    ]

    small = jnp.concatenate(
        [
            halved(attend_vectors).reshape(-1),
            halved(feed_vectors).reshape(-1),
            halved(expand_bias),
        ]
    )
    small_rows = 16
    small_block = jnp.pad(small, (0, small_rows * model_width - small.shape[0])).reshape(
        small_rows, model_width
    )
    out_rows = outward.shape[0]
    first = lax.all_gather(
        jnp.concatenate([halved(outward), small_block], axis=0), whole, axis=0, tiled=True
    ).reshape(devices, out_rows + small_rows, model_width)
    out_whole = first[:, :out_rows].reshape(devices * out_rows, model_width)
    small_all = first[:, out_rows:].reshape(devices, -1)[:, : small.shape[0]].astype(jnp.float32)
    vectors = jnp.transpose(
        small_all[:, : 8 * vec_width].reshape(devices, 8, vec_width), (1, 0, 2)
    ).reshape(8, model_width)
    vec_one = vectors[:5]
    vec_two = vectors[5:]
    bias_all = small_all[:, 8 * vec_width :].reshape(replicas, groups, hidden_part)
    bias_part = lax.dynamic_index_in_dim(bias_all, mine, 1, keepdims=False).reshape(-1)

    in_width = 3 * part_width
    moved_in = spread_columns(halved(inward), groups, part_width)
    moved_up = spread_columns(halved(expand), groups, hidden_part)
    in_part = lax.all_gather(moved_in, "dp", axis=0, tiled=True)
    up_part = lax.all_gather(moved_up, "dp", axis=0, tiled=True)
    down_part = lax.all_gather(halved(shrink), "dp", axis=0, tiled=True)

    cotangent = (output_cotangent * live_mask).reshape(row_count, model_width)
    cot_all = gather_rows(halved(cotangent))
    feed_bias_grad = jnp.sum(cotangent, axis=0)

    flat_tokens = tokens.reshape(row_count, model_width)
    normed_one, inverse_one = normalize(flat_tokens)
    lifted_one = gather_rows(halved(normed_one * vec_one[0] + vec_one[1]))
    packed = jnp.dot(lifted_one, in_part, preferred_element_type=jnp.float32)
    bias_query = lax.dynamic_slice_in_dim(vec_one[2], mine * part_width, part_width)
    bias_value = lax.dynamic_slice_in_dim(vec_one[3], mine * part_width, part_width)

    def to_heads(operand):
        return jnp.transpose(
            operand.reshape(slot_count, length, head_count, HEAD_DIM), (0, 2, 1, 3)
        )

    def from_heads(operand):
        return jnp.transpose(operand, (0, 2, 1, 3)).reshape(all_rows, part_width)

    queries = to_heads(halved(packed[:, :part_width] + bias_query))
    keys = to_heads(halved(packed[:, part_width : 2 * part_width]))
    values = to_heads(halved(packed[:, 2 * part_width :] + bias_value))
    positions = jnp.arange(length)
    allowed = positions[None, :] <= positions[:, None]
    scores = (
        jnp.einsum("shqd,shkd->shqk", queries, keys, preferred_element_type=jnp.float32)
        * score_scale
    )
    scores = jnp.where(allowed, scores, masked_score)
    score_peak = jnp.max(scores, axis=-1, keepdims=True)
    log_total = score_peak + jnp.log(jnp.sum(jnp.exp(scores - score_peak), axis=-1, keepdims=True))
    weights_full = jnp.exp(scores - log_total)
    weights_half = halved(weights_full)
    attended_heads = halved(
        jnp.einsum("shqk,shkd->shqd", weights_half, values, preferred_element_type=jnp.float32)
    )
    attended = lax.all_to_all(
        from_heads(attended_heads).reshape(slot_count, length, part_width), "seq", 1, 2, tiled=True
    ).reshape(row_count, model_width)
    projected = jnp.dot(attended, out_whole, preferred_element_type=jnp.float32)
    middle = flat_tokens + projected + vec_one[4]
    normed_two, inverse_two = normalize(middle)
    lifted_two = gather_rows(halved(normed_two * vec_two[0] + vec_two[1]))
    upper = jnp.dot(lifted_two, up_part, preferred_element_type=jnp.float32) + bias_part
    active_full, slope = gelu_pair(upper)
    active = halved(active_full)
    upper_grad = (
        lax.dot_general(
            cot_all, down_part, (((1,), (1,)), ((), ())), preferred_element_type=jnp.float32
        )
        * slope
    )
    upper_half = halved(upper_grad)
    lift_two_grad = scatter_rows(
        lax.dot_general(
            upper_half, up_part, (((1,), (1,)), ((), ())), preferred_element_type=jnp.float32
        )
    )
    fed = scatter_rows(jnp.dot(active, down_part, preferred_element_type=jnp.float32))
    block_output = (middle + fed + vec_two[2]).reshape(
        slot_count, block_size, model_width
    ) * live_mask

    def outer(left, right):
        return halved(
            lax.dot_general(
                left, right, (((0,), (0,)), ((), ())), preferred_element_type=jnp.float32
            )
        )

    shrink_sum = lax.psum_scatter(
        outer(active, cot_all), "dp", scatter_dimension=0, tiled=True
    ).astype(jnp.float32)
    expand_sum = collect_columns(
        lax.psum_scatter(outer(lifted_two, upper_half), "dp", scatter_dimension=0, tiled=True),
        groups,
        hidden_part,
    ).astype(jnp.float32)
    bias_grad = jnp.sum(upper_grad, axis=0).reshape(replicas, 1, hidden_part)

    gain_two_grad = jnp.sum(lift_two_grad * normed_two, axis=0)
    shift_two_grad = jnp.sum(lift_two_grad, axis=0)
    middle_grad = cotangent + norm_back(lift_two_grad * vec_two[0], normed_two, inverse_two)
    middle_half = halved(middle_grad)
    out_bias_grad = jnp.sum(middle_grad, axis=0)
    attended_back = halved(
        lax.dot_general(
            middle_half, out_whole, (((1,), (1,)), ((), ())), preferred_element_type=jnp.float32
        )
    )
    attended_grad = to_heads(
        lax.all_to_all(
            attended_back.reshape(slot_count, block_size, model_width), "seq", 2, 1, tiled=True
        ).reshape(all_rows, part_width)
    )
    outward_sum = lax.psum_scatter(
        outer(attended, middle_half), whole, scatter_dimension=0, tiled=True
    ).astype(jnp.float32)
    delta_sum = jnp.sum(
        attended_grad.astype(jnp.float32) * attended_heads.astype(jnp.float32),
        axis=-1,
        keepdims=True,
    )
    weight_grad = jnp.einsum(
        "shqd,shkd->shqk", attended_grad, values, preferred_element_type=jnp.float32
    )
    score_grad = halved(weights_full * (weight_grad - delta_sum) * score_scale)
    query_grad = from_heads(
        jnp.einsum("shqk,shkd->shqd", score_grad, keys, preferred_element_type=jnp.float32)
    )
    key_grad = from_heads(
        jnp.einsum("shqk,shqd->shkd", score_grad, queries, preferred_element_type=jnp.float32)
    )
    value_grad = from_heads(
        jnp.einsum(
            "shqk,shqd->shkd", weights_half, attended_grad, preferred_element_type=jnp.float32
        )
    )
    packed_grad = halved(jnp.concatenate([query_grad, key_grad, value_grad], axis=1))
    lift_one_grad = scatter_rows(
        lax.dot_general(
            packed_grad, in_part, (((1,), (1,)), ((), ())), preferred_element_type=jnp.float32
        )
    )
    inward_sum = collect_columns(
        lax.psum_scatter(outer(lifted_one, packed_grad), "dp", scatter_dimension=0, tiled=True),
        groups,
        part_width,
    ).astype(jnp.float32)

    def place_part(part):
        return lax.dynamic_update_slice_in_dim(
            jnp.zeros((model_width,), jnp.float32), part, mine * part_width, 0
        )

    gain_one_grad = jnp.sum(lift_one_grad * normed_one, axis=0)
    shift_one_grad = jnp.sum(lift_one_grad, axis=0)
    tokens_grad = middle_grad + norm_back(lift_one_grad * vec_one[0], normed_one, inverse_one)
    input_gradient = tokens_grad.reshape(slot_count, block_size, model_width) * live_mask
    vector_grads = jnp.stack(
        [
            gain_one_grad,
            shift_one_grad,
            place_part(jnp.sum(query_grad, axis=0)),
            place_part(jnp.sum(value_grad, axis=0)),
            out_bias_grad,
            gain_two_grad,
            shift_two_grad,
            feed_bias_grad,
        ]
    ).T
    bias_placed = lax.dynamic_update_slice_in_dim(
        jnp.zeros((replicas, groups, hidden_part), jnp.float32), bias_grad, mine, 1
    ).reshape(model_width, -1)
    small_sum = lax.psum_scatter(
        jnp.concatenate([vector_grads, bias_placed], axis=1),
        whole,
        scatter_dimension=0,
        tiled=True,
    )
    attend_vec_sum = small_sum[:, :5].T
    feed_vec_sum = small_sum[:, 5:8].T
    bias_sum = small_sum[:, 8:].reshape(-1)
    inward_new, inward_state = adamw_update(inward, inward_sum, inward_moments, weight_decay)
    outward_new, outward_state = adamw_update(outward, outward_sum, outward_moments, weight_decay)
    attend_new, attend_state = adamw_update(attend_vectors, attend_vec_sum, attend_moments, 0.0)
    expand_new, expand_state = adamw_update(expand, expand_sum, expand_moments, weight_decay)
    shrink_new, shrink_state = adamw_update(shrink, shrink_sum, shrink_moments, weight_decay)
    feed_new, feed_state = adamw_update(feed_vectors, feed_vec_sum, feed_moments, 0.0)
    bias_new, bias_state = adamw_update(expand_bias, bias_sum, bias_moments, 0.0)
    return (
        block_output,
        input_gradient,
        inward_sum,
        outward_sum,
        attend_vec_sum,
        expand_sum,
        shrink_sum,
        feed_vec_sum,
        bias_sum,
        inward_new,
        outward_new,
        attend_new,
        expand_new,
        shrink_new,
        feed_new,
        bias_new,
        inward_state,
        outward_state,
        attend_state,
        expand_state,
        shrink_state,
        feed_state,
        bias_state,
    )


def solution(mesh):
    placed = (
        P("dp", "seq", None),
        P("dp", "seq", None),
        P(),
        P(("dp", "seq"), None),
        P(("dp", "seq"), None),
        P(None, ("dp", "seq")),
        P(("dp", "seq"), None),
        P(("dp", "seq"), None),
        P(None, ("dp", "seq")),
        P(("dp", "seq")),
        P(None, ("dp", "seq"), None),
        P(None, ("dp", "seq"), None),
        P(None, None, ("dp", "seq")),
        P(None, ("dp", "seq"), None),
        P(None, ("dp", "seq"), None),
        P(None, None, ("dp", "seq")),
        P(None, ("dp", "seq")),
    )
    return jax.shard_map(
        body,
        mesh=mesh,
        in_specs=placed,
        out_specs=(
            P("dp", "seq", None),
            P("dp", "seq", None),
            P(("dp", "seq"), None),
            P(("dp", "seq"), None),
            P(None, ("dp", "seq")),
            P(("dp", "seq"), None),
            P(("dp", "seq"), None),
            P(None, ("dp", "seq")),
            P(("dp", "seq")),
            P(("dp", "seq"), None),
            P(("dp", "seq"), None),
            P(None, ("dp", "seq")),
            P(("dp", "seq"), None),
            P(("dp", "seq"), None),
            P(None, ("dp", "seq")),
            P(("dp", "seq")),
            P(None, ("dp", "seq"), None),
            P(None, ("dp", "seq"), None),
            P(None, None, ("dp", "seq")),
            P(None, ("dp", "seq"), None),
            P(None, ("dp", "seq"), None),
            P(None, None, ("dp", "seq")),
            P(None, ("dp", "seq")),
        ),
        check_vma=False,
    )
```

time: 1390 us -> 883 us (0.64)
  waiting for transfers between devices: 1070 us -> 723 us
  blocking collectives: 159 us -> 27 us
  matrix products: 74.3 us -> 40.4 us
    reduce_scatter x6 -> x7, waiting for transfers between devices: 697 us -> 380 us  [the longest x1 124 us: body(): lax.psum_scatter(outer(attended, middle_half), whole, scatter_dimension=0...]
    all_gather x3 -> x0, blocking collectives: 120 us -> none  [the longest x1 43.8 us: body(): lax.all_gather(attend_cols, ('dp', 'seq'), axis=0, tiled=True)]
    unnamed x16, waiting for transfers between devices: 192 us -> 123 us
    unnamed x1 -> x0, blocking collectives: 39.4 us -> none
    dot_general x18, matrix products: 74.3 us -> 40.4 us  [the longest x4 13.1 us: outer(): lax.dot_general(left, right, (((0,), (0,)), ((), ())), preferred_element_...]
    all_gather x6 -> x7, waiting for transfers between devices: 179 us -> 208 us  [the longest x1 50.3 us: body(): lax.all_gather(jnp.concatenate([halved(outward), small_block], axis=0), w...]
    all_to_all x0 -> x3, blocking collectives: none -> 27 us  [the longest x2 17.9 us: spread_columns(): moved = lax.all_to_all(parts, 'seq', 2, 0, tiled=True)]
  transfers between devices with their start and end apart: 14 -> 18, of which waited for: 11 -> 18; matrix products, arithmetic and copies ran while one was open for 6% -> 7% of each run, Pallas kernels for 0% -> 0%
where the time goes in v1:
time: 883 us; the launch traced here: 882 us
  waiting for transfers between devices  723 us (82%)
  matrix products  40.4 us (5%)
  local copies, waits for them, and re-layouts  33.8 us (4%)
  other arithmetic  31 us (4%)
  blocking collectives  27 us (3%)
  between operations  15 us (2%)
  starting transfers between devices  11.4 us (1%)
    reduce_scatter x1, waiting for transfers between devices, body(): lax.psum_scatter(outer(attended, middle_half), whole, scatter_dimension=0...  124 us
    unnamed x16, waiting for transfers between devices  123 us
    reduce_scatter x1, waiting for transfers between devices, body(): lax.psum_scatter(outer(active, cot_all), 'dp', scatter_dimension=0, tiled...  68.5 us
    reduce_scatter x3, waiting for transfers between devices, scatter_rows(): lax.psum_scatter(halved(partial).reshape(slot_count, length, -1), 'seq',...  64.8 us
    reduce_scatter x1, waiting for transfers between devices, body(): lax.psum_scatter(outer(lifted_two, upper_half), 'dp', scatter_dimension=0...  62.3 us
    reduce_scatter x1, waiting for transfers between devices, body(): lax.psum_scatter(outer(lifted_one, packed_grad), 'dp', scatter_dimension=...  60.3 us
    all_gather x1, waiting for transfers between devices, body(): lax.all_gather(jnp.concatenate([halved(outward), small_block], axis=0), w...  50.3 us
    all_gather x3, waiting for transfers between devices, gather_rows(): lax.all_gather(local.reshape(slot_count, block_size, -1), 'seq', axis=1,...  48.7 us
  transfers between devices with their start and end apart: 18, of which 18 were waited for; matrix products, arithmetic and copies ran while one was open for 7% of the time, Pallas kernels for 0%

profile of v1, /device:TPU:0, one launch (start us, length us, event | category | flops | bytes accessed | tf_op | source)
XLA Modules:
  0.0 881.6 jit_solution(11967319726546057766)
XLA Ops:
  12.4 9.4 %all_to_all.78 = bf16[32,3,4,256]{3,0,1,2:T(8,128)(2,1)S(1)} all-to-all(bf16[32,3,4,256]{3,0,1,2:T(8,128)(2,1)S(1)} %copy.236), channel_id=1, replica_groups=mesh['dp'=8,'seq'=4] {'seq'}, dimensions={2} | all-to-all | bytes 393216 | tf_op jit(solution)/shard_map/all_to_all | solution.py:64
  23.1 50.3 %all-gather.8.cloned.1.call-done = bf16[1536,1024]{1,0:T(8,128)(2,1)} async-done(((bf16[48,1024]{1,0:T(8,128)(2,1)}), bf16[1536,1024]{1,0:T(8,128)(2,1)}) %all-gather.8.cloned.1.call-update) | async-done | bytes 3145744 | tf_op jit(solution)/shard_map/all_gather | solution.py:138
  77.6 8.5 all_to_all.79
  87.3 31.8 %all-gather.12.cloned.1.call-done = bf16[1024,768]{1,0:T(8,128)(2,1)} async-done(((bf16[128,768]{1,0:T(8,128)(2,1)}), bf16[1024,768]{1,0:T(8,128)(2,1)}) %all-gather.12.cloned.1.call-update) | async-done | bytes 1572880 | tf_op jit(solution)/shard_map/all_gather | solution.py:154
  119.1 17.2 %all-gather.10.cloned.1.call-done = bf16[2,256,1024]{2,1,0:T(8,128)(2,1)} async-done(((bf16[2,64,1024]{2,1,0:T(8,128)(2,1)}), bf16[2,256,1024]{2,1,0:T(8,128)(2,1)}) %all-gather.10.cloned.1.call-update) | async-done | bytes 1048592 | tf_op jit(solution)/shard_map/all_gather | solution.py:110
  136.3 2.7 fusion.89
  142.3 3.4 all-to-all-start.1
  145.8 3.3 slice.165
  158.5 29.5 %all-gather.16.cloned.1.call-done = bf16[1024,1024]{1,0:T(8,128)(2,1)} async-done(((bf16[128,1024]{1,0:T(8,128)(2,1)}), bf16[1024,1024]{1,0:T(8,128)(2,1)}) %all-gather.16.cloned.1.call-update) | async-done | bytes 2097168 | tf_op jit(solution)/shard_map/all_gather | solution.py:155
  188.0 17.3 %all-gather.14.cloned.1.call-done = bf16[2,256,1024]{2,1,0:T(8,128)(2,1)} async-done(((bf16[2,64,1024]{2,1,0:T(8,128)(2,1)}), bf16[2,256,1024]{2,1,0:T(8,128)(2,1)}) %all-gather.14.cloned.1.call-update) | async-done | bytes 1048592 | tf_op jit(solution)/shard_map/all_gather | solution.py:110
  205.3 4.5 fusion.90
  209.8 14.2 %all-gather.20.cloned.1.call-done = bf16[2,256,1024]{2,1,0:T(8,128)(2,1)} async-done(((bf16[2,64,1024]{2,1,0:T(8,128)(2,1)}), bf16[2,256,1024]{2,1,0:T(8,128)(2,1)}) %all-gather.20.cloned.1.call-update) | async-done | bytes 1048592 | tf_op jit(solution)/shard_map/all_gather | solution.py:110
  224.0 4.9 convolution_convert_fusion
  229.0 68.5 %reduce-scatter.23.cloned.1.call-done = bf16[128,1024]{1,0:T(8,128)(2,1)} async-done(((bf16[1024,1024]{1,0:T(8,128)(2,1)}), bf16[128,1024]{1,0:T(8,128)(2,1)}) %reduce-scatter.23.cloned.1.call-update) | async-done | bytes 262160 | tf_op jit(solution)/shard_map/reduce_scatter | solution.py:228
  301.4 48.0 %all-gather.18.cloned.1.call-done = bf16[1024,1024]{1,0:T(8,128)(2,1)} async-done(((bf16[128,1024]{1,0:T(8,128)(2,1)}), bf16[1024,1024]{1,0:T(8,128)(2,1)}) %all-gather.18.cloned.1.call-update) | async-done | bytes 2097168 | tf_op jit(solution)/shard_map/all_gather | solution.py:156
  349.4 5.1 fusion.88
  356.9 4.7 convolution_convert_fusion.6
  361.7 18.6 %reduce-scatter.13.cloned.1.call-done = bf16[2,64,1024]{2,1,0:T(8,128)(2,1)} async-done(((bf16[2,256,1024]{2,1,0:T(8,128)(2,1)}), bf16[2,64,1024]{2,1,0:T(8,128)(2,1)}) %reduce-scatter.13.cloned.1.call-update) | async-done | bytes 262160 | tf_op jit(solution)/shard_map/reduce_scatter | solution.py:116
  382.7 25.3 %reduce-scatter.11.cloned.1.call-done = bf16[2,64,1024]{2,1,0:T(8,128)(2,1)} async-done(((bf16[2,256,1024]{2,1,0:T(8,128)(2,1)}), bf16[2,64,1024]{2,1,0:T(8,128)(2,1)}) %reduce-scatter.11.cloned.1.call-update) | async-done | bytes 262160 | tf_op jit(solution)/shard_map/reduce_scatter | solution.py:116
  408.0 2.4 fusion.81
  413.8 9.1 %all_to_all.80 = bf16[4,2,16384]{2,1,0:T(2,128)(2,1)} all-to-all(bf16[4,2,16384]{2,1,0:T(2,128)(2,1)S(1)} %reshape.573), channel_id=1, replica_groups=mesh['dp'=8,'seq'=4] {'seq'}, dimensions={0} | all-to-all | bytes 524288 | tf_op jit(solution)/shard_map/all_to_all | solution.py:249
  435.1 2.6 convolution_convert_fusion.1
  438.8 21.0 %reduce-scatter.15.cloned.1.call-done = bf16[2,64,1024]{2,1,0:T(8,128)(2,1)} async-done(((bf16[2,256,1024]{2,1,0:T(8,128)(2,1)}), bf16[2,64,1024]{2,1,0:T(8,128)(2,1)}) %reduce-scatter.15.cloned.1.call-update) | async-done | bytes 262160 | tf_op jit(solution)/shard_map/reduce_scatter | solution.py:116
  462.2 3.5 convolution_convert_fusion.3
  469.2 62.3 %reduce-scatter.21.cloned.1.call-done = bf16[128,1024]{1,0:T(8,128)(2,1)} async-done(((bf16[1024,1024]{1,0:T(8,128)(2,1)}), bf16[128,1024]{1,0:T(8,128)(2,1)}) %reduce-scatter.21.cloned.1.call-update) | async-done | bytes 262160 | tf_op jit(solution)/shard_map/reduce_scatter | solution.py:232
  533.1 3.4 all-to-all-start.5
  538.1 4.5 all-to-all-done.5
  545.9 122.6 %reduce-scatter.25.cloned.1.call-done = f32[32,12]{1,0:T(8,128)} async-done(((f32[1024,12]{1,0:T(8,128)}), f32[32,12]{1,0:T(8,128)}) %reduce-scatter.25.cloned.1.call-update) | async-done | bytes 1552
  673.0 60.3 %reduce-scatter.17.cloned.1.call-done = bf16[128,768]{1,0:T(8,128)(2,1)} async-done(((bf16[1024,768]{1,0:T(8,128)(2,1)}), bf16[128,768]{1,0:T(8,128)(2,1)}) %reduce-scatter.17.cloned.1.call-update) | async-done | bytes 196624 | tf_op jit(solution)/shard_map/reduce_scatter | solution.py:283
  735.3 3.5 all-to-all-start.4
  740.6 4.9 all-to-all-done.4
  748.5 124.2 %reduce-scatter.19.cloned.1.call-done = bf16[32,1024]{1,0:T(8,128)(2,1)} async-done(((bf16[1024,1024]{1,0:T(8,128)(2,1)}), bf16[32,1024]{1,0:T(8,128)(2,1)}) %reduce-scatter.19.cloned.1.call-update) | async-done | bytes 65552 | tf_op jit(solution)/shard_map/reduce_scatter | solution.py:253
  (289 shorter events, 75.0 us)
Async XLA Ops:
  7.2 15.6 %copy-start.1 = (f32[2,64,1024]{2,1,0:T(8,128)S(1)}, f32[2,64,1024]{2,1,0:T(8,128)}, u32[]{:S(2)}) copy-start(f32[2,64,1024]{2,1,0:T(8,128)} %param.17) | copy-start | bytes 1572868
  7.2 66.2 %all-gather.8.cloned.1.call-start = ((), (), s32[]{:S(2)}) async-start(), calls=%async_computation.14 | async-start | bytes 3244032 | tf_op jit(solution)/shard_map/all_gather | solution.py:138
  11.2 107.9 %all-gather.12.cloned.1.call-start = ((), (), s32[]{:S(2)}) async-start(), calls=%async_computation.16 | async-start | bytes 1769472 | tf_op jit(solution)/shard_map/all_gather | solution.py:154
  22.7 113.6 %all-gather.10.cloned.1.call-start = ((), (), s32[]{:S(2)}) async-start(), calls=%async_computation.15 | async-start | bytes 1310720 | tf_op jit(solution)/shard_map/all_gather | solution.py:110
  77.3 110.7 %all-gather.16.cloned.1.call-start = ((), (), s32[]{:S(2)}) async-start(), calls=%async_computation.18 | async-start | bytes 2359296 | tf_op jit(solution)/shard_map/all_gather | solution.py:155
  142.3 9.4 %all-to-all-start.1 = ((bf16[2,256,256]{2,0,1:T(2,128)(2,1)}), bf16[2,256,256]{2,0,1:T(2,128)(2,1)S(1)}, u32[]{:S(2)}, u32[]{:S(2)}) async-start(bf16[2,256,256]{2,0,1:T(2,128)(2,1)} %copy.245), calls=%async_computation.1 | async-start | bytes 524288 | tf_op jit(solution)/shard_map/all_to_all | solution.py:194
  145.8 59.5 %all-gather.14.cloned.1.call-start = ((), (), s32[]{:S(2)}) async-start(), calls=%async_computation.17 | async-start | bytes 1310720 | tf_op jit(solution)/shard_map/all_gather | solution.py:110
  155.4 68.6 %all-gather.20.cloned.1.call-start = ((), (), s32[]{:S(2)}) async-start(), calls=%async_computation.21 | async-start | bytes 1310720 | tf_op jit(solution)/shard_map/all_gather | solution.py:110
  158.4 139.1 %reduce-scatter.23.cloned.1.call-start = ((), (), s32[]{:S(2)}) async-start(), calls=%async_computation.27 | async-start | bytes 2359296 | tf_op jit(solution)/shard_map/reduce_scatter | solution.py:228
  228.9 120.5 %all-gather.18.cloned.1.call-start = ((), (), s32[]{:S(2)}) async-start(), calls=%async_computation.19 | async-start | bytes 2359296 | tf_op jit(solution)/shard_map/all_gather | solution.py:156
  301.2 79.1 %reduce-scatter.13.cloned.1.call-start = ((), (), s32[]{:S(2)}) async-start(), calls=%async_computation.22 | async-start | bytes 1310720 | tf_op jit(solution)/shard_map/reduce_scatter | solution.py:116
  356.8 51.2 %reduce-scatter.11.cloned.1.call-start = ((), (), s32[]{:S(2)}) async-start(), calls=%async_computation.20 | async-start | bytes 1310720 | tf_op jit(solution)/shard_map/reduce_scatter | solution.py:116
  361.6 98.2 %reduce-scatter.15.cloned.1.call-start = ((), (), s32[]{:S(2)}) async-start(), calls=%async_computation.23 | async-start | bytes 1310720 | tf_op jit(solution)/shard_map/reduce_scatter | solution.py:116
  412.3 16.4 %copy-start.9 = (bf16[2,4,256,64]{2,3,1,0:T(8,128)(2,1)S(1)}, bf16[2,4,256,64]{2,3,1,0:T(8,128)(2,1)}, u32[]{:S(2)}) copy-start(bf16[2,4,256,64]{2,3,1,0:T(8,128)(2,1)} %copy-done.8) | copy-start | bytes 786436
  434.8 96.7 %reduce-scatter.21.cloned.1.call-start = ((), (), s32[]{:S(2)}) async-start(), calls=%async_computation.26 | async-start | bytes 2359296 | tf_op jit(solution)/shard_map/reduce_scatter | solution.py:232
  437.7 24.5 %copy-start.31 = (bf16[512,768]{0,1:T(8,128)(2,1)S(1)}, bf16[512,768]{0,1:T(8,128)(2,1)}, u32[]{:S(2)}) copy-start(bf16[512,768]{0,1:T(8,128)(2,1)} %copy-done.30) | copy-start | bytes 2359300
  437.7 230.8 %reduce-scatter.25.cloned.1.call-start = ((), (), s32[]{:S(2)}) async-start(), calls=%async_computation.28 | async-start | bytes 540672
  462.2 271.2 %reduce-scatter.17.cloned.1.call-start = ((), (), s32[]{:S(2)}) async-start(), calls=%async_computation.24 | async-start | bytes 1769472 | tf_op jit(solution)/shard_map/reduce_scatter | solution.py:283
  465.8 406.9 %reduce-scatter.19.cloned.1.call-start = ((), (), s32[]{:S(2)}) async-start(), calls=%async_computation.25 | async-start | bytes 2162688 | tf_op jit(solution)/shard_map/reduce_scatter | solution.py:253
  469.1 67.6 %copy-start.25 = (bf16[2,64,1024]{2,1,0:T(8,128)(2,1)S(1)}, bf16[2,64,1024]{2,1,0:T(8,128)(2,1)}, u32[]{:S(2)}) copy-start(bf16[2,64,1024]{2,1,0:T(8,128)(2,1)} %reduce-scatter.15.cloned.1.call-done) | copy-start | bytes 786436
  469.1 67.8 %copy-start.21 = (f32[128,1024]{1,0:T(8,128)S(1)}, f32[128,1024]{1,0:T(8,128)}, u32[]{:S(2)}) copy-start(f32[128,1024]{1,0:T(8,128)} %get-tuple-element.221) | copy-start | bytes 1572868
  533.1 9.5 %all-to-all-start.5 = ((bf16[128,8,1,128]{3,1,2,0:T(8,128)(2,1)}), bf16[128,8,1,128]{3,1,2,0:T(8,128)(2,1)S(1)}, u32[]{:S(2)}, u32[]{:S(2)}) async-start(bf16[128,8,1,128]{3,1,2,0:T(8,128)(2,1)} %bitcast.49), calls=%async_computation.11 | async-start | bytes 524288 | tf_op jit(solution)/shard_map/all_to_all | solution.py:71
  543.6 127.6 %copy-start.36 = (f32[5,32]{1,0:T(8,128)S(1)}, f32[5,32]{1,0:T(8,128)}, u32[]{:S(2)}) copy-start(f32[5,32]{1,0:T(8,128)} %param.22) | copy-start | bytes 1924
  543.7 128.2 %copy-start.40 = (f32[2,128]{1,0:T(2,128)S(1)}, f32[2,128]{1,0:T(2,128)}, u32[]{:S(2)}) copy-start(f32[2,128]{1,0:T(2,128)} %param.33) | copy-start | bytes 3076
  543.7 128.2 %copy-start.43 = (f32[128]{0:T(128)S(1)}, f32[128]{0:T(128)}, u32[]{:S(2)}) copy-start(f32[128]{0:T(128)} %param.26) | copy-start | bytes 1540
  543.7 128.8 %copy-start.38 = (f32[3,32]{1,0:T(4,128)S(1)}, f32[3,32]{1,0:T(4,128)}, u32[]{:S(2)}) copy-start(f32[3,32]{1,0:T(4,128)} %param.25) | copy-start | bytes 1156
  669.4 76.6 %copy-start.42 = (f32[128]{0:T(128)}, f32[128]{0:T(128)S(1)}, u32[]{:S(2)}) copy-start(f32[128]{0:T(128)S(1)} %reshape.514) | copy-start | bytes 1540
  670.4 76.0 %copy-start.35 = (f32[32,5]{0,1:T(8,128)}, f32[32,5]{0,1:T(8,128)S(1)}, u32[]{:S(2)}) copy-start(f32[32,5]{0,1:T(8,128)S(1)} %copy.292) | copy-start | bytes 1924
  671.2 75.1 %copy-start.37 = (f32[32,3]{0,1:T(4,128)}, f32[32,3]{0,1:T(4,128)S(1)}, u32[]{:S(2)}) copy-start(f32[32,3]{0,1:T(4,128)S(1)} %copy.293) | copy-start | bytes 1156
  735.3 10.2 %all-to-all-start.4 = ((bf16[128,3,1,256]{3,1,2,0:T(4,128)(2,1)}), bf16[128,3,1,256]{3,1,2,0:T(4,128)(2,1)S(1)}, u32[]{:S(2)}, u32[]{:S(2)}) async-start(bf16[128,3,1,256]{3,1,2,0:T(4,128)(2,1)} %copy.263), calls=%async_computation.8 | async-start | bytes 524288 | tf_op jit(solution)/shard_map/all_to_all | solution.py:71
  746.5 126.2 %copy-start.26 = (f32[2,32,1024]{2,1,0:T(8,128)S(1)}, f32[2,32,1024]{2,1,0:T(8,128)}, u32[]{:S(2)}) copy-start(f32[2,32,1024]{2,1,0:T(8,128)} %param.28) | copy-start | bytes 786436
  746.5 127.1 %copy-start.28 = (f32[32,1024]{1,0:T(8,128)S(1)}, f32[32,1024]{1,0:T(8,128)}, u32[]{:S(2)}) copy-start(f32[32,1024]{1,0:T(8,128)} %param.21) | copy-start | bytes 393220
  (36 other events, 98.6 us)
Sparse Core Ops, SparseCore 0:
  11.5 61.8 all-gather.7
  76.2 42.8 all-gather.11
  121.2 15.0 all-gather.9
  138.9 49.0 all-gather.15
  190.0 15.2 all-gather.13
  207.3 16.6 all-gather.19
  229.1 68.4 reduce-scatter.22
  301.3 48.1 all-gather.17
  356.9 23.2 reduce-scatter.12
  383.2 24.7 reduce-scatter.10
  434.9 24.8 reduce-scatter.14
  463.1 68.2 reduce-scatter.20
  533.7 134.8 reduce-scatter.24
  671.8 61.4 reduce-scatter.16
  735.4 137.2 reduce-scatter.18

commit v2 on v1

--- a/solution.py
+++ b/solution.py
@@ -56,13 +56,6 @@
     unbiased_second = second / (1.0 - beta_second**adam_steps)
     update = unbiased_first / (jnp.sqrt(unbiased_second) + adam_epsilon) + decay_rate * parameter
     return (parameter - learn_rate * update, jnp.stack([first_moment, second]))
-
-
-def spread_columns(piece, groups, inner):
-    rows = piece.shape[0]
-    parts = piece.reshape(rows, -1, groups, inner)
-    moved = lax.all_to_all(parts, "seq", 2, 0, tiled=True)
-    return moved.reshape(groups * rows, -1)
 
 
 def collect_columns(piece, groups, inner):
@@ -104,7 +97,6 @@
     vec_width = attend_vectors.shape[1]
     hidden_part = expand_bias.shape[0]
     score_scale = 1.0 / math.sqrt(HEAD_DIM)
-    whole = ("dp", "seq")
 
     def gather_rows(local):
         full = lax.all_gather(
@@ -130,16 +122,49 @@
             halved(expand_bias),
         ]
     )
-    small_rows = 16
-    small_block = jnp.pad(small, (0, small_rows * model_width - small.shape[0])).reshape(
-        small_rows, model_width
-    )
-    out_rows = outward.shape[0]
+    small_size = small.shape[0]
+    pad_rows = 16
+    in_rows = inward.shape[0]
+    block_rows = groups * in_rows
+    small_row = jnp.broadcast_to(
+        jnp.pad(small, (0, model_width - small_size)), (groups, 1, model_width)
+    )
+    both = jnp.concatenate([halved(inward), halved(outward)], axis=1)
+    both_parts = jnp.transpose(both.reshape(in_rows, -1, groups, part_width), (2, 0, 1, 3))
+    up_parts = jnp.transpose(
+        halved(expand).reshape(in_rows, replicas, groups, hidden_part), (2, 0, 1, 3)
+    )
+    moved = lax.all_to_all(
+        jnp.concatenate(
+            [
+                both_parts.reshape(groups, in_rows, model_width),
+                up_parts.reshape(groups, in_rows, model_width),
+                small_row,
+            ],
+            axis=1,
+        ),
+        "seq",
+        0,
+        0,
+        tiled=True,
+    )
+    small_block = jnp.pad(moved[:, 2 * in_rows], ((0, pad_rows - groups), (0, 0)))
     first = lax.all_gather(
-        jnp.concatenate([halved(outward), small_block], axis=0), whole, axis=0, tiled=True
-    ).reshape(devices, out_rows + small_rows, model_width)
-    out_whole = first[:, :out_rows].reshape(devices * out_rows, model_width)
-    small_all = first[:, out_rows:].reshape(devices, -1)[:, : small.shape[0]].astype(jnp.float32)
+        jnp.concatenate(
+            [moved[:, :in_rows].reshape(block_rows, model_width), small_block], axis=0
+        ),
+        "dp",
+        axis=0,
+        tiled=True,
+    ).reshape(replicas, block_rows + pad_rows, model_width)
+    both_part = first[:, :block_rows].reshape(model_width, model_width)
+    in_part = both_part[:, : 3 * part_width]
+    out_part = both_part[:, 3 * part_width :]
+    small_all = (
+        first[:, block_rows : block_rows + groups, :small_size]
+        .reshape(devices, small_size)
+        .astype(jnp.float32)
+    )
     vectors = jnp.transpose(
         small_all[:, : 8 * vec_width].reshape(devices, 8, vec_width), (1, 0, 2)
     ).reshape(8, model_width)
@@ -147,12 +172,12 @@
     vec_two = vectors[5:]
     bias_all = small_all[:, 8 * vec_width :].reshape(replicas, groups, hidden_part)
     bias_part = lax.dynamic_index_in_dim(bias_all, mine, 1, keepdims=False).reshape(-1)
-
-    in_width = 3 * part_width
-    moved_in = spread_columns(halved(inward), groups, part_width)
-    moved_up = spread_columns(halved(expand), groups, hidden_part)
-    in_part = lax.all_gather(moved_in, "dp", axis=0, tiled=True)
-    up_part = lax.all_gather(moved_up, "dp", axis=0, tiled=True)
+    up_part = lax.all_gather(
+        moved[:, in_rows : 2 * in_rows].reshape(block_rows, model_width),
+        "dp",
+        axis=0,
+        tiled=True,
+    )
     down_part = lax.all_gather(halved(shrink), "dp", axis=0, tiled=True)
 
     cotangent = (output_cotangent * live_mask).reshape(row_count, model_width)
@@ -191,10 +216,17 @@
     attended_heads = halved(
         jnp.einsum("shqk,shkd->shqd", weights_half, values, preferred_element_type=jnp.float32)
     )
-    attended = lax.all_to_all(
-        from_heads(attended_heads).reshape(slot_count, length, part_width), "seq", 1, 2, tiled=True
+    attended = lax.all_gather(from_heads(attended_heads), "seq", axis=0, tiled=False)
+    attended = jnp.transpose(attended, (1, 0, 2)).reshape(all_rows, model_width)
+    projected = lax.all_to_all(
+        halved(jnp.dot(attended, out_part, preferred_element_type=jnp.float32)).reshape(
+            slot_count, length, part_width
+        ),
+        "seq",
+        1,
+        2,
+        tiled=True,
     ).reshape(row_count, model_width)
-    projected = jnp.dot(attended, out_whole, preferred_element_type=jnp.float32)
     middle = flat_tokens + projected + vec_one[4]
     normed_two, inverse_two = normalize(middle)
     lifted_two = gather_rows(halved(normed_two * vec_two[0] + vec_two[1]))
@@ -240,19 +272,23 @@
     middle_grad = cotangent + norm_back(lift_two_grad * vec_two[0], normed_two, inverse_two)
     middle_half = halved(middle_grad)
     out_bias_grad = jnp.sum(middle_grad, axis=0)
+    middle_cols = lax.all_to_all(
+        middle_half.reshape(slot_count, block_size, model_width), "seq", 2, 1, tiled=True
+    ).reshape(all_rows, part_width)
     attended_back = halved(
         lax.dot_general(
-            middle_half, out_whole, (((1,), (1,)), ((), ())), preferred_element_type=jnp.float32
+            middle_cols, out_part, (((1,), (1,)), ((), ())), preferred_element_type=jnp.float32
         )
     )
     attended_grad = to_heads(
-        lax.all_to_all(
-            attended_back.reshape(slot_count, block_size, model_width), "seq", 2, 1, tiled=True
+        lax.psum_scatter(
+            jnp.transpose(attended_back.reshape(all_rows, groups, part_width), (1, 0, 2)),
+            "seq",
+            scatter_dimension=0,
+            tiled=True,
         ).reshape(all_rows, part_width)
     )
-    outward_sum = lax.psum_scatter(
-        outer(attended, middle_half), whole, scatter_dimension=0, tiled=True
-    ).astype(jnp.float32)
+    outward_part = outer(attended, middle_cols)
     delta_sum = jnp.sum(
         attended_grad.astype(jnp.float32) * attended_heads.astype(jnp.float32),
         axis=-1,
@@ -279,11 +315,7 @@
             packed_grad, in_part, (((1,), (1,)), ((), ())), preferred_element_type=jnp.float32
         )
     )
-    inward_sum = collect_columns(
-        lax.psum_scatter(outer(lifted_one, packed_grad), "dp", scatter_dimension=0, tiled=True),
-        groups,
-        part_width,
-    ).astype(jnp.float32)
+    inward_part = outer(lifted_one, packed_grad)
 
     def place_part(part):
         return lax.dynamic_update_slice_in_dim(
@@ -305,19 +337,51 @@
             shift_two_grad,
             feed_bias_grad,
         ]
-    ).T
+    ).reshape(8, devices, vec_width)
     bias_placed = lax.dynamic_update_slice_in_dim(
         jnp.zeros((replicas, groups, hidden_part), jnp.float32), bias_grad, mine, 1
-    ).reshape(model_width, -1)
-    small_sum = lax.psum_scatter(
-        jnp.concatenate([vector_grads, bias_placed], axis=1),
-        whole,
+    ).reshape(devices, hidden_part)
+    small_grads = halved(
+        jnp.concatenate(
+            [jnp.transpose(vector_grads, (1, 0, 2)).reshape(devices, 8 * vec_width), bias_placed],
+            axis=1,
+        )
+    ).reshape(replicas, groups, small_size)
+    small_grads = jnp.pad(
+        small_grads, ((0, 0), (0, pad_rows - groups), (0, model_width - small_size))
+    )
+    both_grads = jnp.concatenate([inward_part, outward_part], axis=1).reshape(
+        replicas, block_rows, model_width
+    )
+    reduced = lax.psum_scatter(
+        jnp.concatenate([both_grads, small_grads], axis=1).reshape(-1, model_width),
+        "dp",
         scatter_dimension=0,
         tiled=True,
     )
-    attend_vec_sum = small_sum[:, :5].T
-    feed_vec_sum = small_sum[:, 5:8].T
-    bias_sum = small_sum[:, 8:].reshape(-1)
+    returned = lax.all_to_all(
+        jnp.concatenate(
+            [
+                reduced[:block_rows].reshape(groups, in_rows, model_width),
+                reduced[block_rows : block_rows + groups].reshape(groups, 1, model_width),
+            ],
+            axis=1,
+        ),
+        "seq",
+        0,
+        0,
+        tiled=True,
+    )
+    both_sum = jnp.transpose(
+        returned[:, :in_rows].reshape(groups, in_rows, -1, part_width), (1, 2, 0, 3)
+    ).reshape(in_rows, -1).astype(jnp.float32)
+    inward_sum = both_sum[:, : 3 * model_width]
+    outward_sum = both_sum[:, 3 * model_width :]
+    small_sum = jnp.sum(returned[:, in_rows, :small_size].astype(jnp.float32), axis=0)
+    vector_sum = small_sum[: 8 * vec_width].reshape(8, vec_width)
+    attend_vec_sum = vector_sum[:5]
+    feed_vec_sum = vector_sum[5:]
+    bias_sum = small_sum[8 * vec_width :]
     inward_new, inward_state = adamw_update(inward, inward_sum, inward_moments, weight_decay)
     outward_new, outward_state = adamw_update(outward, outward_sum, outward_moments, weight_decay)
     attend_new, attend_state = adamw_update(attend_vectors, attend_vec_sum, attend_moments, 0.0)

time: 883 us -> 655 us (0.74)
  waiting for transfers between devices: 723 us -> 471 us
  local copies, waits for them, and re-layouts: 33.8 us -> 50.9 us
  other arithmetic: 31 us -> 40.6 us
    unnamed x16 -> x14, waiting for transfers between devices: 123 us -> 0.74 us
    reduce_scatter x2, waiting for transfers between devices: 185 us -> 82.6 us  [the longest x1 57.8 us: body(): lax.psum_scatter(jnp.concatenate([both_grads, small_grads], axis=1).resha...]
    all_gather x3, waiting for transfers between devices: 112 us -> 95.3 us  [the longest x1 51.9 us: body(): lax.all_gather(jnp.concatenate([moved[:, :in_rows].reshape(block_rows, mo...]
    reduce_scatter x3, waiting for transfers between devices: 64.8 us -> 51.7 us  [scatter_rows(): lax.psum_scatter(halved(partial).reshape(slot_count, length, -1), 'seq',...]
    all_to_all x3 -> x2, blocking collectives: 27 us -> 23.8 us  [the longest x1 13.7 us: body(): lax.all_to_all(jnp.concatenate([both_parts.reshape(groups, in_rows, model...]
  transfers between devices with their start and end apart: 18 -> 17, of which waited for: 18 -> 17; matrix products, arithmetic and copies ran while one was open for 7% -> 9% of each run, Pallas kernels for 0% -> 0%
where the time goes in v2:
time: 655 us; the launch traced here: 653 us
  waiting for transfers between devices  471 us (72%)
  local copies, waits for them, and re-layouts  50.9 us (8%)
  other arithmetic  40.6 us (6%)
  matrix products  40.5 us (6%)
  blocking collectives  23.8 us (4%)
  between operations  15.1 us (2%)
  starting transfers between devices  11.3 us (2%)
    reduce_scatter x1, waiting for transfers between devices, body(): lax.psum_scatter(outer(active, cot_all), 'dp', scatter_dimension=0, tiled...  68.6 us
    reduce_scatter x1, waiting for transfers between devices, body(): lax.psum_scatter(outer(lifted_two, upper_half), 'dp', scatter_dimension=0...  66.1 us
    reduce_scatter x1, waiting for transfers between devices, body(): lax.psum_scatter(jnp.concatenate([both_grads, small_grads], axis=1).resha...  57.8 us
    all_gather x1, waiting for transfers between devices, body(): lax.all_gather(jnp.concatenate([moved[:, :in_rows].reshape(block_rows, mo...  51.9 us
    reduce_scatter x3, waiting for transfers between devices, scatter_rows(): lax.psum_scatter(halved(partial).reshape(slot_count, length, -1), 'seq',...  51.7 us
    all_gather x1, waiting for transfers between devices, body(): down_part = lax.all_gather(halved(shrink), 'dp', axis=0, tiled=True)  48 us
    all_gather x3, waiting for transfers between devices, gather_rows(): lax.all_gather(local.reshape(slot_count, block_size, -1), 'seq', axis=1,...  43.9 us
    all_gather x1, waiting for transfers between devices, body(): lax.all_gather(moved[:, in_rows:2 * in_rows].reshape(block_rows, model_wi...  27.1 us
  transfers between devices with their start and end apart: 17, of which 17 were waited for; matrix products, arithmetic and copies ran while one was open for 9% of the time, Pallas kernels for 0%

profile of v2, /device:TPU:0, one launch (start us, length us, event | category | flops | bytes accessed | tf_op | source)
XLA Modules:
  0.0 653.0 jit_solution(9173827048181499504)
XLA Ops:
  11.7 13.7 %all_to_all.43 = bf16[4,65,1024]{2,1,0:T(8,128)(2,1)S(1)} all-to-all(bf16[4,65,1024]{2,1,0:T(8,128)(2,1)S(1)} %pad_maximum_fusion.5), channel_id=1, replica_groups=mesh['dp'=8,'seq'=4] {'seq'}, dimensions={0} | all-to-all | bytes 1064960 | tf_op jit(solution)/shard_map/all_to_all | solution.py:137
  27.3 51.9 %all-gather.8.cloned.1.call-done = bf16[1152,1024]{1,0:T(8,128)(2,1)} async-done(((bf16[144,1024]{1,0:T(8,128)(2,1)}), bf16[1152,1024]{1,0:T(8,128)(2,1)}) %all-gather.8.cloned.1.call-update) | async-done | bytes 2359312 | tf_op jit(solution)/shard_map/all_gather | solution.py:152
  85.6 12.5 %all-gather.10.cloned.1.call-done = bf16[2,256,1024]{2,1,0:T(8,128)(2,1)} async-done(((bf16[2,64,1024]{2,1,0:T(8,128)(2,1)}), bf16[2,256,1024]{2,1,0:T(8,128)(2,1)}) %all-gather.10.cloned.1.call-update) | async-done | bytes 1048592 | tf_op jit(solution)/shard_map/all_gather | solution.py:102
  109.8 16.3 %all-gather.12.cloned.1.call-done = bf16[4,512,256]{2,1,0:T(8,128)(2,1)} async-done(((bf16[1,512,256]{2,1,0:T(8,128)(2,1)}), bf16[4,512,256]{2,1,0:T(8,128)(2,1)}) %all-gather.12.cloned.1.call-update) | async-done | bytes 1048592 | tf_op jit(solution)/shard_map/all_gather | solution.py:219
  126.0 2.3 copy.226
  131.2 3.4 all-to-all-start.1
  136.6 3.9 all-to-all-done.1
  150.7 27.1 %all-gather.16.cloned.1.call-done = bf16[1024,1024]{1,0:T(8,128)(2,1)} async-done(((bf16[128,1024]{1,0:T(8,128)(2,1)}), bf16[1024,1024]{1,0:T(8,128)(2,1)}) %all-gather.16.cloned.1.call-update) | async-done | bytes 2097168 | tf_op jit(solution)/shard_map/all_gather | solution.py:175
  177.9 17.3 %all-gather.14.cloned.1.call-done = bf16[2,256,1024]{2,1,0:T(8,128)(2,1)} async-done(((bf16[2,64,1024]{2,1,0:T(8,128)(2,1)}), bf16[2,256,1024]{2,1,0:T(8,128)(2,1)}) %all-gather.14.cloned.1.call-update) | async-done | bytes 1048592 | tf_op jit(solution)/shard_map/all_gather | solution.py:102
  195.1 4.6 fusion.111
  199.7 14.2 %all-gather.20.cloned.1.call-done = bf16[2,256,1024]{2,1,0:T(8,128)(2,1)} async-done(((bf16[2,64,1024]{2,1,0:T(8,128)(2,1)}), bf16[2,256,1024]{2,1,0:T(8,128)(2,1)}) %all-gather.20.cloned.1.call-update) | async-done | bytes 1048592 | tf_op jit(solution)/shard_map/all_gather | solution.py:102
  213.8 4.9 convolution_convert_fusion
  218.8 68.6 %reduce-scatter.20.cloned.1.call-done = bf16[128,1024]{1,0:T(8,128)(2,1)} async-done(((bf16[1024,1024]{1,0:T(8,128)(2,1)}), bf16[128,1024]{1,0:T(8,128)(2,1)}) %reduce-scatter.20.cloned.1.call-update) | async-done | bytes 262160 | tf_op jit(solution)/shard_map/reduce_scatter | solution.py:260
  291.3 48.0 %all-gather.18.cloned.1.call-done = bf16[1024,1024]{1,0:T(8,128)(2,1)} async-done(((bf16[128,1024]{1,0:T(8,128)(2,1)}), bf16[1024,1024]{1,0:T(8,128)(2,1)}) %all-gather.18.cloned.1.call-update) | async-done | bytes 2097168 | tf_op jit(solution)/shard_map/all_gather | solution.py:181
  339.3 5.7 fusion.110
  347.4 4.7 convolution_convert_fusion.6
  352.9 17.8 %reduce-scatter.10.cloned.1.call-done = bf16[2,64,1024]{2,1,0:T(8,128)(2,1)} async-done(((bf16[2,256,1024]{2,1,0:T(8,128)(2,1)}), bf16[2,64,1024]{2,1,0:T(8,128)(2,1)}) %reduce-scatter.10.cloned.1.call-update) | async-done | bytes 262160 | tf_op jit(solution)/shard_map/reduce_scatter | solution.py:108
  373.2 24.8 %reduce-scatter.8.cloned.1.call-done = bf16[2,64,1024]{2,1,0:T(8,128)(2,1)} async-done(((bf16[2,256,1024]{2,1,0:T(8,128)(2,1)}), bf16[2,64,1024]{2,1,0:T(8,128)(2,1)}) %reduce-scatter.8.cloned.1.call-update) | async-done | bytes 262160 | tf_op jit(solution)/shard_map/reduce_scatter | solution.py:108
  398.0 2.9 fusion.101
  404.8 10.1 %all_to_all.44 = bf16[4,2,16384]{2,1,0:T(2,128)(2,1)} all-to-all(bf16[4,2,16384]{2,1,0:T(2,128)(2,1)} %reshape.857), channel_id=1, replica_groups=mesh['dp'=8,'seq'=4] {'seq'}, dimensions={0} | all-to-all | bytes 524288 | tf_op jit(solution)/shard_map/all_to_all | solution.py:275
  418.3 2.6 convolution_convert_fusion.4
  420.9 2.3 copy.266
  423.3 24.9 %reduce-scatter.12.cloned.1.call-done = bf16[1,512,256]{1,2,0:T(8,128)(2,1)} async-done(((bf16[4,512,256]{1,2,0:T(8,128)(2,1)}), bf16[1,512,256]{1,2,0:T(8,128)(2,1)}) %reduce-scatter.12.cloned.1.call-update) | async-done | bytes 262160 | tf_op jit(solution)/shard_map/reduce_scatter | solution.py:284
  456.3 2.6 convolution_convert_fusion.1
  469.0 2.9 copy.267
  471.9 9.0 %reduce-scatter.14.cloned.1.call-done = bf16[2,64,1024]{2,1,0:T(8,128)(2,1)} async-done(((bf16[2,256,1024]{2,1,0:T(8,128)(2,1)}), bf16[2,64,1024]{2,1,0:T(8,128)(2,1)}) %reduce-scatter.14.cloned.1.call-update) | async-done | bytes 262160 | tf_op jit(solution)/shard_map/reduce_scatter | solution.py:108
  486.7 66.1 %reduce-scatter.18.cloned.1.call-done = bf16[128,1024]{1,0:T(8,128)(2,1)} async-done(((bf16[1024,1024]{1,0:T(8,128)(2,1)}), bf16[128,1024]{1,0:T(8,128)(2,1)}) %reduce-scatter.18.cloned.1.call-update) | async-done | bytes 262160 | tf_op jit(solution)/shard_map/reduce_scatter | solution.py:264
  554.5 3.4 all-to-all-start.4
  559.5 4.3 all-to-all-done.4
  567.2 57.8 %reduce-scatter.16.cloned.1.call-done = bf16[144,1024]{1,0:T(8,128)(2,1)} async-done(((bf16[1152,1024]{1,0:T(8,128)(2,1)}), bf16[144,1024]{1,0:T(8,128)(2,1)}) %reduce-scatter.16.cloned.1.call-update) | async-done | bytes 294928 | tf_op jit(solution)/shard_map/reduce_scatter | solution.py:356
  627.4 3.5 all-to-all-start.3
  632.0 5.6 all-to-all-done.3
  (376 shorter events, 98.3 us)
Async XLA Ops:
  7.2 72.0 %all-gather.8.cloned.1.call-start = ((), (), s32[]{:S(2)}) async-start(), calls=%async_computation.12 | async-start | bytes 2654208 | tf_op jit(solution)/shard_map/all_gather | solution.py:152
  26.9 71.1 %all-gather.10.cloned.1.call-start = ((), (), s32[]{:S(2)}) async-start(), calls=%async_computation.13 | async-start | bytes 1310720 | tf_op jit(solution)/shard_map/all_gather | solution.py:102
  27.1 58.1 %copy-start.48 = (f32[2,64]{1,0:T(2,128)}, f32[2,64]{1,0:T(2,128)S(1)}, u32[]{:S(2)}) copy-start(f32[2,64]{1,0:T(2,128)S(1)} %broadcast_multiply_fusion.5) | copy-start | bytes 1540
  27.3 57.9 %copy-start.52 = (f32[2,64]{1,0:T(2,128)}, f32[2,64]{1,0:T(2,128)S(1)}, u32[]{:S(2)}) copy-start(f32[2,64]{1,0:T(2,128)S(1)} %add_rsqrt_fusion.1) | copy-start | bytes 1540
  82.6 43.4 %all-gather.12.cloned.1.call-start = ((), (), s32[]{:S(2)}) async-start(), calls=%async_computation.14 | async-start | bytes 1310720 | tf_op jit(solution)/shard_map/all_gather | solution.py:219
  105.9 22.4 %copy-start.7 = (bf16[2,4,256,64]{2,3,1,0:T(8,128)(2,1)}, bf16[2,4,256,64]{2,3,1,0:T(8,128)(2,1)S(1)}, u32[]{:S(2)}) copy-start(bf16[2,4,256,64]{2,3,1,0:T(8,128)(2,1)S(1)} %convolution_convert_fusion.8) | copy-start | bytes 786436
  109.2 68.7 %all-gather.16.cloned.1.call-start = ((), (), s32[]{:S(2)}) async-start(), calls=%async_computation.16 | async-start | bytes 2359296 | tf_op jit(solution)/shard_map/all_gather | solution.py:175
  131.2 9.4 %all-to-all-start.1 = ((bf16[2,256,256]{2,0,1:T(2,128)(2,1)}), bf16[2,256,256]{2,0,1:T(2,128)(2,1)S(1)}, u32[]{:S(2)}, u32[]{:S(2)}) async-start(bf16[2,256,256]{2,0,1:T(2,128)(2,1)} %copy.227), calls=%async_computation.1 | async-start | bytes 524288 | tf_op jit(solution)/shard_map/all_to_all | solution.py:221
  134.6 60.5 %all-gather.14.cloned.1.call-start = ((), (), s32[]{:S(2)}) async-start(), calls=%async_computation.15 | async-start | bytes 1310720 | tf_op jit(solution)/shard_map/all_gather | solution.py:102
  146.7 67.1 %all-gather.20.cloned.1.call-start = ((), (), s32[]{:S(2)}) async-start(), calls=%async_computation.19 | async-start | bytes 1310720 | tf_op jit(solution)/shard_map/all_gather | solution.py:102
  150.1 137.4 %reduce-scatter.20.cloned.1.call-start = ((), (), s32[]{:S(2)}) async-start(), calls=%async_computation.25 | async-start | bytes 2359296 | tf_op jit(solution)/shard_map/reduce_scatter | solution.py:260
  218.8 120.6 %all-gather.18.cloned.1.call-start = ((), (), s32[]{:S(2)}) async-start(), calls=%async_computation.17 | async-start | bytes 2359296 | tf_op jit(solution)/shard_map/all_gather | solution.py:181
  291.0 79.7 %reduce-scatter.10.cloned.1.call-start = ((), (), s32[]{:S(2)}) async-start(), calls=%async_computation.20 | async-start | bytes 1310720 | tf_op jit(solution)/shard_map/reduce_scatter | solution.py:108
  347.3 23.5 %copy-start.39 = (f32[1024]{0:T(1024)S(1)}, f32[1024]{0:T(1024)}, u32[]{:S(2)}) copy-start(f32[1024]{0:T(1024)} %mul.617) | copy-start | bytes 12292
  347.3 23.5 %copy-start.51 = (f32[2,64]{1,0:T(2,128)S(1)}, f32[2,64]{1,0:T(2,128)}, u32[]{:S(2)}) copy-start(f32[2,64]{1,0:T(2,128)} %copy-done.50) | copy-start | bytes 1540
  347.3 23.5 %copy-start.56 = (f32[2,64]{1,0:T(2,128)S(1)}, f32[2,64]{1,0:T(2,128)}, u32[]{:S(2)}) copy-start(f32[2,64]{1,0:T(2,128)} %copy-done.55) | copy-start | bytes 1540
  347.3 50.6 %reduce-scatter.8.cloned.1.call-start = ((), (), s32[]{:S(2)}) async-start(), calls=%async_computation.18 | async-start | bytes 1310720 | tf_op jit(solution)/shard_map/reduce_scatter | solution.py:108
  352.1 96.0 %reduce-scatter.12.cloned.1.call-start = ((), (), s32[]{:S(2)}) async-start(), calls=%async_computation.21 | async-start | bytes 1310720 | tf_op jit(solution)/shard_map/reduce_scatter | solution.py:284
  420.9 28.3 %copy-start.8 = (bf16[2,4,256,64]{2,3,1,0:T(8,128)(2,1)S(1)}, bf16[2,4,256,64]{2,3,1,0:T(8,128)(2,1)}, u32[]{:S(2)}) copy-start(bf16[2,4,256,64]{2,3,1,0:T(8,128)(2,1)} %copy-done.7) | copy-start | bytes 786436
  420.9 28.4 %copy-start.35 = (f32[1,8,256]{2,1,0:T(8,128)S(1)}, f32[1,8,256]{2,1,0:T(8,128)}, u32[]{:S(2)}) copy-start(f32[1,8,256]{2,1,0:T(8,128)} %copy-done.34) | copy-start | bytes 24580
  423.2 57.7 %reduce-scatter.14.cloned.1.call-start = ((), (), s32[]{:S(2)}) async-start(), calls=%async_computation.22 | async-start | bytes 1310720 | tf_op jit(solution)/shard_map/reduce_scatter | solution.py:108
  456.0 96.8 %reduce-scatter.18.cloned.1.call-start = ((), (), s32[]{:S(2)}) async-start(), calls=%async_computation.24 | async-start | bytes 2359296 | tf_op jit(solution)/shard_map/reduce_scatter | solution.py:264
  459.0 166.0 %reduce-scatter.16.cloned.1.call-start = ((), (), s32[]{:S(2)}) async-start(), calls=%async_computation.23 | async-start | bytes 2654208 | tf_op jit(solution)/shard_map/reduce_scatter | solution.py:356
  486.0 71.9 %copy-start.74 = (f32[2,3,32]{2,0,1:T(2,128)S(1)}, f32[2,3,32]{2,0,1:T(2,128)}, u32[]{:S(2)}) copy-start(f32[2,3,32]{2,0,1:T(2,128)} %param.32) | copy-start | bytes 2308
  486.0 72.5 %copy-start.21 = (f32[1,128,1024]{2,1,0:T(8,128)S(1)}, f32[1,128,1024]{2,1,0:T(8,128)}, u32[]{:S(2)}) copy-start(f32[1,128,1024]{2,1,0:T(8,128)} %get-tuple-element.177) | copy-start | bytes 1572868
  486.0 72.5 %copy-start.22 = (f32[1,128,1024]{2,1,0:T(8,128)S(1)}, f32[1,128,1024]{2,1,0:T(8,128)}, u32[]{:S(2)}) copy-start(f32[1,128,1024]{2,1,0:T(8,128)} %get-tuple-element.187) | copy-start | bytes 1572868
  554.5 9.4 %all-to-all-start.4 = ((bf16[128,8,1,128]{3,1,2,0:T(8,128)(2,1)}), bf16[128,8,1,128]{3,1,2,0:T(8,128)(2,1)S(1)}, u32[]{:S(2)}, u32[]{:S(2)}) async-start(bf16[128,8,1,128]{3,1,2,0:T(8,128)(2,1)} %bitcast.42), calls=%async_computation.10 | async-start | bytes 524288 | tf_op jit(solution)/shard_map/all_to_all | solution.py:64
  565.9 65.0 %copy-start.2 = (f32[2,64,1024]{2,1,0:T(8,128)S(1)}, f32[2,64,1024]{2,1,0:T(8,128)}, u32[]{:S(2)}) copy-start(f32[2,64,1024]{2,1,0:T(8,128)} %copy-done.1) | copy-start | bytes 1572868
  565.9 65.0 %copy-start.13 = (bf16[2,64,1024]{2,1,0:T(8,128)(2,1)S(1)}, bf16[2,64,1024]{2,1,0:T(8,128)(2,1)}, u32[]{:S(2)}) copy-start(bf16[2,64,1024]{2,1,0:T(8,128)(2,1)} %reduce-scatter.14.cloned.1.call-done) | copy-start | bytes 786436
  565.9 65.0 %copy-start.54 = (f32[2,64]{1,0:T(2,128)S(1)}, f32[2,64]{1,0:T(2,128)}, u32[]{:S(2)}) copy-start(f32[2,64]{1,0:T(2,128)} %copy-done.52) | copy-start | bytes 1540
  566.0 65.0 %copy-start.69 = (f32[2]{0:T(128)S(1)}, f32[2]{0:T(128)}, u32[]{:S(2)}) copy-start(f32[2]{0:T(128)} %copy-done.68) | copy-start | bytes 28
  627.4 10.1 %all-to-all-start.3 = ((bf16[4,33,1024]{2,1,0:T(8,128)(2,1)}), bf16[4,33,1024]{2,1,0:T(8,128)(2,1)S(1)}, u32[]{:S(2)}, u32[]{:S(2)}) async-start(bf16[4,33,1024]{2,1,0:T(8,128)(2,1)} %pad_maximum_fusion.6), calls=%async_computation.8 | async-start | bytes 655360 | tf_op jit(solution)/shard_map/all_to_all | solution.py:362
  (68 other events, 329.7 us)
Sparse Core Ops, SparseCore 0:
  27.1 52.0 all-gather.7
  82.8 15.2 all-gather.9
  109.3 16.6 all-gather.11
  128.6 49.2 all-gather.15
  179.8 15.2 all-gather.13
  197.1 16.6 all-gather.19
  218.9 68.4 reduce-scatter.19
  291.2 48.1 all-gather.17
  347.4 23.3 reduce-scatter.9
  373.1 24.7 reduce-scatter.7
  423.3 24.7 reduce-scatter.11
  456.1 24.8 reduce-scatter.13
  484.5 68.2 reduce-scatter.17
  556.1 68.8 reduce-scatter.15
